TPU v7x, 512 devices: a whole 4x8x8 slice. The times are simulated.
512 devices in a mesh: dp: 16 (over y_lo, x), tile: 32 (over y_hi, z, core).
Axes of the slice: x: 4, y: 8 (y_hi: 2, y_lo: 4; y = y_hi * 4 + y_lo), z: 8, core: 2. Of those that a mesh axis runs over, the one named last changes fastest.
Arguments:
- features: bfloat16 [16, 32, 8, 16, 1024], P('dp', 'tile'), may hold values from -6 to 6
- cotangent: bfloat16 [16, 32, 8, 16, 1024], P('dp', 'tile'), may hold values from -6 to 6
- in_weight: bfloat16 [3072, 1024], P(('dp', 'tile')), may hold values from -0.1875 to 0.1875
- out_weight: bfloat16 [3072, 1024], P(('dp', 'tile')), may hold values from -0.109375 to 0.109375
- hidden_bias: bfloat16 [3072], P(('dp', 'tile')), may hold values from -3 to 3
- kernel: float32 [49, 1024], P(None, 'dp'), may hold values from -0.875 to 0.875
- conv_bias: float32 [1024], P('dp'), may hold values from -3 to 3
- norm_gain: float32 [1024], P('dp'), may hold values from 0.5 to 1.5
- norm_bias: float32 [1024], P('dp'), may hold values from -3 to 3
- layer_scale: float32 [1024], P('dp'), may hold values from 0.5 to 1.5
- out_bias: float32 [1024], P('dp'), may hold values from -3 to 3
Outputs:
- block_out: bfloat16 [16, 32, 8, 16, 1024], P('dp', 'tile')
- grad_input: bfloat16 [16, 32, 8, 16, 1024], P('dp', 'tile')
- grad_kernel: float32 [49, 1024], P(None, 'dp')
- grad_conv_bias: float32 [1024], P('dp')
- grad_norm_gain: float32 [1024], P('dp')
- grad_norm_bias: float32 [1024], P('dp')
- grad_layer_scale: float32 [1024], P('dp')
All inputs are finite; a program needn't handle non-finite values.
Results may differ from a plain program's by a relative error of at most 0.0061.
Values may be sent and summed in bfloat16 or wider, within the bound.
A program may use at most 128 MiB of HBM per device.

v0:
```python
import math

import jax
import jax.numpy as jnp
from jax import lax
from jax.sharding import PartitionSpec as P

KS = 7
GX = 4


def passed_along(block, axis, distance):
    devices = range(lax.axis_size(axis))
    route = [(i - distance, i) for i in devices if i - distance in devices]
    return lax.ppermute(block, axis, route)


def gelu_exact(values):
    return 0.5 * values * (1.0 + jax.scipy.special.erf(values * 0.7071067811865476))


def gelu_slope(values):
    return (
        0.5 * (1.0 + jax.scipy.special.erf(values * 0.7071067811865476))
        + values * jnp.exp(-0.5 * values * values) * 0.3989422804014327
    )


def edge_part(field, step, axis):
    length = field.shape[axis]
    margin = KS // 2
    if step < 0:
        return lax.slice_in_dim(field, length - margin, length, axis=axis)
    if step > 0:
        return lax.slice_in_dim(field, 0, margin, axis=axis)
    return field


def pad_field(field, row_place, col_place, grid_rows):
    bands = []
    for row_step in (-1, 0, 1):
        pieces = []
        for col_step in (-1, 0, 1):
            if row_step == 0 and col_step == 0:
                pieces.append(field)
            else:
                border = edge_part(edge_part(field, row_step, 1), col_step, 2)
                moved = passed_along(border, "tile", -(row_step * GX + col_step))
                row_new = row_place + row_step
                col_new = col_place + col_step
                pieces.append(
                    jnp.where(
                        (row_new >= 0) & (row_new < grid_rows) & (col_new >= 0) & (col_new < GX),
                        moved,
                        jnp.zeros_like(moved),
                    )
                )
        bands.append(jnp.concatenate(pieces, axis=2))
    return jnp.concatenate(bands, axis=1)


def per_device(
    features,
    cotangent,
    in_weight,
    out_weight,
    hidden_bias,
    kernel,
    conv_bias,
    norm_gain,
    norm_bias,
    layer_scale,
    out_bias,
):
    image_count, _, rows, cols, width = features.shape
    tile_count = lax.axis_size("tile")
    grid_rows = tile_count // GX
    place = lax.axis_index("tile")
    row_place = place // GX
    col_place = place % GX
    margin = KS // 2
    kernel_all, cbias, gain, nbias, lscale, obias = (
        lax.all_gather(kernel, "dp", axis=1, tiled=True),
        lax.all_gather(conv_bias, "dp", axis=0, tiled=True),
        lax.all_gather(norm_gain, "dp", axis=0, tiled=True),
        lax.all_gather(norm_bias, "dp", axis=0, tiled=True),
        lax.all_gather(layer_scale, "dp", axis=0, tiled=True),
        lax.all_gather(out_bias, "dp", axis=0, tiled=True),
    )
    picture = features.reshape(image_count, rows, cols, width)
    padded = pad_field(picture, row_place, col_place, grid_rows)
    convolved = jnp.zeros((image_count, rows, cols, width), jnp.float32) + cbias
    for tap_row in range(KS):
        for tap_col in range(KS):
            window = padded[:, tap_row : tap_row + rows, tap_col : tap_col + cols, :].astype(
                jnp.float32
            )
            convolved = convolved + kernel_all[tap_row * KS + tap_col] * window
    average = jnp.mean(convolved, axis=-1, keepdims=True)
    centered = convolved - average
    variance = jnp.mean(centered * centered, axis=-1, keepdims=True)
    inverse = lax.rsqrt(variance + 1e-06)
    pixel_rows = image_count * rows * cols
    standard = (centered * inverse).reshape(pixel_rows, width)
    inverse = inverse.reshape(pixel_rows, 1)
    normed = (standard * gain + nbias).astype(jnp.bfloat16)
    upstream = cotangent.reshape(pixel_rows, width).astype(jnp.float32)
    back_out = (upstream * lscale).astype(jnp.bfloat16)
    rows_in = lax.all_gather(in_weight, ("dp", "tile"), axis=0, tiled=True)
    rows_out = lax.all_gather(out_weight, ("dp", "tile"), axis=0, tiled=True)
    bias_part = lax.all_gather(hidden_bias, ("dp", "tile"), axis=0, tiled=True)
    pre = lax.dot_general(
        normed, rows_in, (((1,), (1,)), ((), ())), preferred_element_type=jnp.float32
    ) + bias_part.astype(jnp.float32)
    hidden = gelu_exact(pre).astype(jnp.bfloat16)
    mlp_sum = jnp.dot(hidden, rows_out, preferred_element_type=jnp.float32)
    back_hidden = lax.dot_general(
        back_out, rows_out, (((1,), (1,)), ((), ())), preferred_element_type=jnp.float32
    )
    back_pre = (back_hidden * gelu_slope(pre)).astype(jnp.bfloat16)
    normed_sum = jnp.dot(back_pre, rows_in, preferred_element_type=jnp.float32)
    mlp_sum, back_normed = (mlp_sum, normed_sum)
    projected = mlp_sum + obias
    source = picture.reshape(pixel_rows, width).astype(jnp.float32)
    block_out = (source + lscale * projected).astype(jnp.bfloat16).reshape(features.shape)
    scale_part = jnp.sum(upstream * projected, axis=0)
    gain_part = jnp.sum(back_normed * standard, axis=0)
    nbias_part = jnp.sum(back_normed, axis=0)
    scaled = back_normed * gain
    back_conv = inverse * (
        scaled
        - jnp.mean(scaled, axis=-1, keepdims=True)
        - standard * jnp.mean(scaled * standard, axis=-1, keepdims=True)
    )
    cbias_part = jnp.sum(back_conv, axis=0)
    back_grid = back_conv.reshape(image_count, rows, cols, width)
    back_padded = pad_field(back_grid.astype(jnp.bfloat16), row_place, col_place, grid_rows)
    grad_grid = upstream.reshape(image_count, rows, cols, width)
    kernel_rows = []
    for tap_row in range(KS):
        for tap_col in range(KS):
            tap_weight = kernel_all[tap_row * KS + tap_col]
            flipped = back_padded[
                :,
                2 * margin - tap_row : 2 * margin - tap_row + rows,
                2 * margin - tap_col : 2 * margin - tap_col + cols,
                :,
            ].astype(jnp.float32)
            grad_grid = grad_grid + tap_weight * flipped
            window = padded[:, tap_row : tap_row + rows, tap_col : tap_col + cols, :].astype(
                jnp.float32
            )
            kernel_rows.append(jnp.sum(back_grid * window, axis=(0, 1, 2)))
    grad_input = grad_grid.astype(jnp.bfloat16).reshape(features.shape)
    kernel_terms = jnp.stack(kernel_rows)
    shared = (
        lax.psum_scatter(kernel_terms, "dp", scatter_dimension=1, tiled=True),
        lax.psum_scatter(cbias_part, "dp", scatter_dimension=0, tiled=True),
        lax.psum_scatter(gain_part, "dp", scatter_dimension=0, tiled=True),
        lax.psum_scatter(nbias_part, "dp", scatter_dimension=0, tiled=True),
        lax.psum_scatter(scale_part, "dp", scatter_dimension=0, tiled=True),
    )
    kernel_sum, cbias_sum, gain_sum, nbias_sum, scale_sum = lax.psum(
        (shared[0], shared[1], shared[2], shared[3], shared[4]), "tile"
    )
    factor = 1.0 / math.sqrt(image_count * lax.axis_size("dp") * rows * cols * tile_count)
    return (
        block_out,
        grad_input,
        kernel_sum * factor,
        cbias_sum * factor,
        gain_sum * factor,
        nbias_sum * factor,
        scale_sum * factor,
    )


def solution(mesh):
    placed = (
        P("dp", "tile", None, None, None),
        P("dp", "tile", None, None, None),
        P(("dp", "tile"), None),
        P(("dp", "tile"), None),
        P(("dp", "tile")),
        P(None, "dp"),
        P("dp"),
        P("dp"),
        P("dp"),
        P("dp"),
        P("dp"),
    )
    return jax.shard_map(
        per_device,
        mesh=mesh,
        in_specs=placed,
        out_specs=(
            P("dp", "tile", None, None, None),
            P("dp", "tile", None, None, None),
            P(None, "dp"),
            P("dp"),
            P("dp"),
            P("dp"),
            P("dp"),
        ),
        check_vma=False,
    )
```

profile of v0, /device:TPU:2, one launch (start us, length us, event | category | flops | bytes accessed | tf_op | source)
XLA Modules:
  0.0 2040.9 jit_solution(7205430439878918634)
XLA Ops:
  9.6 5.5 collective-permute-start
  15.2 1.3 collective-permute-start.7
  16.5 1.3 collective-permute-start.5
  17.8 8.3 collective-permute-start.2
  27.2 1.7 collective-permute-start.3
  29.0 40.8 %all-gather = f32[16,64,49]{1,2,0:T(8,128)S(1)} all-gather(f32[1,64,49]{1,2,0:T(8,128)} %bitcast.363), channel_id=1, replica_groups=mesh['dp'=16,'tile'=32] {'dp'}, dimensions={0}, use_global_device_ids=true | all-gather | bytes 213248 | tf_op jit(solution)/shard_map/all_gather | solution.py:83
  71.5 109.4 %all-reduce.4 = bf16[3072]{0:T(1024)(128)(2,1)S(1)} all-reduce(bf16[3072]{0:T(1024)(128)(2,1)S(1)} %dynamic-update-slice.4), channel_id=1, replica_groups=mesh['dp'=16,'tile'=32] {'dp','tile'}, use_global_device_ids=true, to_apply=%add.4 | all-reduce | flops 3072 | bytes 12288
  183.9 70.2 %all-reduce.12 = (f32[1024]{0:T(1024)S(1)}, f32[1024]{0:T(1024)S(1)}, f32[1024]{0:T(1024)}, f32[1024]{0:T(1024)}, f32[1024]{0:T(1024)}) all-reduce(f32[1024]{0:T(1024)S(1)} %dynamic-update-slice.1, f32[1024]{0:T(1024)S(1)} %dynamic-update-slice.3, f32[1024]{0:T(1024)S(1)} %dynamic-update-slice.2, ...), channel_id=1, replica_groups=mesh['dp'=16,'tile'=32] {'dp'}, use_global_device_ids=true, to_apply=%add.1 | all-reduce | flops 5120 | bytes 40960
  255.5 2.4 collective-permute-start.1
  257.9 1.3 collective-permute-start.6
  260.6 7.4 collective-permute-done.6
  268.6 6.5 fusion.155
  276.2 1.4 fusion.135
  277.6 558.1 %all-gather.6.cloned.1.call-done = bf16[512,6,1024]{2,1,0:T(8,128)(2,1)} async-done(((bf16[1,6,1024]{2,1,0:T(8,128)(2,1)}), bf16[512,6,1024]{2,1,0:T(8,128)(2,1)}) %all-gather.6.cloned.1.call-update) | async-done | bytes 6291472 | tf_op jit(solution)/shard_map/all_gather | solution.py:109
  835.8 11.0 reshape.319
  846.8 5.1 convolution_add_fusion
  851.9 804.8 %all-gather.8.cloned.1.call-done = bf16[512,6,1024]{2,1,0:T(8,128)(2,1)} async-done(((bf16[1,6,1024]{2,1,0:T(8,128)(2,1)}), bf16[512,6,1024]{2,1,0:T(8,128)(2,1)}) %all-gather.8.cloned.1.call-update) | async-done | bytes 6291472 | tf_op jit(solution)/shard_map/all_gather | solution.py:110
  1656.8 11.1 reshape.321
  1667.8 5.3 fusion.133
  1673.1 9.4 fusion.139
  1682.5 2.4 fusion.103
  1687.3 1.3 collective-permute-start.10
  1688.7 72.7 %all-reduce.11 = (f32[1024]{0:T(1024)S(1)}, f32[1024]{0:T(1024)S(1)}, f32[1024]{0:T(1024)S(1)}, f32[1024]{0:T(1024)S(1)}) all-reduce(f32[1024]{0:T(1024)S(1)} %get-tuple-element.62, f32[1024]{0:T(1024)S(1)} %copy-done.83, f32[1024]{0:T(1024)S(1)} %copy-done.84, f32[1024]{0:T(1024)S(1)} %copy-done.80), channel_id=3, replica_groups=mesh['dp'=16,'tile'=32] {'dp'}, use_global_device_ids=true, to_apply=%region_56.57.clone | all-reduce | flops 4096 | bytes 32768
  1763.0 9.5 collective-permute-start.15
  1772.5 1.3 collective-permute-start.12
  1773.8 1.3 collective-permute-start.8
  1776.9 1.3 collective-permute-start.9
  1779.6 7.4 collective-permute-start.14
  1787.2 3.3 collective-permute-done.11
  1791.2 5.7 fusion.148
  1797.0 66.6 %reduce-scatter.4.cloned.1.call-done = f32[64,49]{1,0:T(8,128)} async-done(((f32[1024,49]{1,0:T(8,128)}), f32[64,49]{1,0:T(8,128)}) %reduce-scatter.4.cloned.1.call-update) | async-done | bytes 12560
  1864.5 167.2 %all-reduce.10 = (f32[49,64]{1,0:T(8,128)S(1)}, f32[64]{0:T(128)S(1)}, f32[64]{0:T(128)S(1)}, f32[64]{0:T(128)S(1)}, f32[64]{0:T(128)S(1)}) all-reduce(f32[49,64]{1,0:T(8,128)S(1)} %copy.21, f32[64]{0:T(128)S(1)} %dynamic-slice.6, f32[64]{0:T(128)S(1)} %dynamic-slice.8, ...), channel_id=1, replica_groups=mesh['dp'=16,'tile'=32] {'tile'}, use_global_device_ids=true, to_apply=%region_54.55 | all-reduce | flops 3392 | bytes 27136 | tf_op jit(solution)/shard_map/psum | solution.py:163
  (272 shorter events, 21.5 us)
Async XLA Ops:
  7.2 828.6 %all-gather.6.cloned.1.call-start = ((), (), s32[]{:S(2)}) async-start(), calls=%async_computation.1 | async-start | bytes 8404992 | tf_op jit(solution)/shard_map/all_gather | solution.py:109
  7.9 1648.9 %all-gather.8.cloned.1.call-start = ((), (), s32[]{:S(2)}) async-start(), calls=%async_computation.2 | async-start | bytes 8404992 | tf_op jit(solution)/shard_map/all_gather | solution.py:110
  8.7 1855.0 %reduce-scatter.4.cloned.1.call-start = ((), (), s32[]{:S(2)}) async-start(), calls=%async_computation.3 | async-start | bytes 557056
  9.6 244.5 %collective-permute-start = (bf16[1,3,3,1024]{3,2,1,0:T(4,128)(2,1)S(1)}, bf16[1,3,3,1024]{3,2,1,0:T(4,128)(2,1)S(1)}, u32[]{:S(2)}, u32[]{:S(2)}) collective-permute-start(bf16[1,3,3,1024]{3,2,1,0:T(4,128)(2,1)S(1)} %get-tuple-element.105), channel_id=1, source_target_pairs={{0,5},{1,6},{2,7},{3,8},{4,9},{5,10},{6,11},{7,12},{8,13},{9,14},{... | collective-permute-start | bytes 55304 | tf_op jit(solution)/shard_map/ppermute | solution.py:15
  15.2 240.3 %collective-permute-start.7 = (bf16[1,3,3,1024]{3,2,1,0:T(4,128)(2,1)S(1)}, bf16[1,3,3,1024]{3,2,1,0:T(4,128)(2,1)S(1)}, u32[]{:S(2)}, u32[]{:S(2)}) collective-permute-start(bf16[1,3,3,1024]{3,2,1,0:T(4,128)(2,1)S(1)} %get-tuple-element.106), channel_id=1, source_target_pairs={{5,0},{6,1},{7,2},{8,3},{9,4},{10,5},{11,6},{12,7},{13,8},{14,9},{... | collective-permute-start | bytes 55304 | tf_op jit(solution)/shard_map/ppermute | solution.py:15
  16.5 241.4 %collective-permute-start.5 = (bf16[1,3,3,1024]{3,2,1,0:T(4,128)(2,1)S(1)}, bf16[1,3,3,1024]{3,2,1,0:T(4,128)(2,1)S(1)}, u32[]{:S(2)}, u32[]{:S(2)}) collective-permute-start(bf16[1,3,3,1024]{3,2,1,0:T(4,128)(2,1)S(1)} %get-tuple-element.107), channel_id=1, source_target_pairs={{3,0},{4,1},{5,2},{6,3},{7,4},{8,5},{9,6},{10,7},{11,8},{12,9},{13... | collective-permute-start | bytes 55304 | tf_op jit(solution)/shard_map/ppermute | solution.py:15
  17.8 241.4 %collective-permute-start.2 = (bf16[1,3,3,1024]{3,2,1,0:T(4,128)(2,1)S(1)}, bf16[1,3,3,1024]{3,2,1,0:T(4,128)(2,1)S(1)}, u32[]{:S(2)}, u32[]{:S(2)}) collective-permute-start(bf16[1,3,3,1024]{3,2,1,0:T(4,128)(2,1)S(1)} %get-tuple-element.108), channel_id=1, source_target_pairs={{0,3},{1,4},{2,5},{3,6},{4,7},{5,8},{6,9},{7,10},{8,11},{9,12},{10... | collective-permute-start | bytes 55304 | tf_op jit(solution)/shard_map/ppermute | solution.py:15
  27.2 232.1 %collective-permute-start.3 = (bf16[1,8,3,1024]{3,2,1,0:T(4,128)(2,1)S(1)}, bf16[1,8,3,1024]{3,2,1,0:T(4,128)(2,1)S(1)}, u32[]{:S(2)}, u32[]{:S(2)}) collective-permute-start(bf16[1,8,3,1024]{3,2,1,0:T(4,128)(2,1)S(1)} %get-tuple-element.111), channel_id=1, source_target_pairs={{0,1},{1,2},{2,3},{3,4},{4,5},{5,6},{6,7},{7,8},{8,9},{9,10},{10,1... | collective-permute-start | bytes 147464 | tf_op jit(solution)/shard_map/ppermute | solution.py:15
  70.1 198.3 %copy-start.4 = (f32[1,1024]{1,0:T(1,128)}, f32[1,1024]{1,0:T(1,128)S(1)}, u32[]{:S(2)}) copy-start(f32[1,1024]{1,0:T(1,128)S(1)} %get-tuple-element.141) | copy-start | bytes 12292
  70.1 198.3 %copy-start.6 = (f32[1,1024]{1,0:T(1,128)}, f32[1,1024]{1,0:T(1,128)S(1)}, u32[]{:S(2)}) copy-start(f32[1,1024]{1,0:T(1,128)S(1)} %get-tuple-element.142) | copy-start | bytes 12292
  71.1 204.0 %copy-start.62 = (f32[1,1024]{1,0:T(1,128)}, f32[1,1024]{1,0:T(1,128)S(1)}, u32[]{:S(2)}) copy-start(f32[1,1024]{1,0:T(1,128)S(1)} %get-tuple-element.151) | copy-start | bytes 12292
  71.1 204.0 %copy-start.64 = (f32[1,1024]{1,0:T(1,128)}, f32[1,1024]{1,0:T(1,128)S(1)}, u32[]{:S(2)}) copy-start(f32[1,1024]{1,0:T(1,128)S(1)} %get-tuple-element.152) | copy-start | bytes 12292
  71.1 204.0 %copy-start.66 = (f32[1,1024]{1,0:T(1,128)}, f32[1,1024]{1,0:T(1,128)S(1)}, u32[]{:S(2)}) copy-start(f32[1,1024]{1,0:T(1,128)S(1)} %get-tuple-element.153) | copy-start | bytes 12292
  71.1 204.1 %copy-start.68 = (f32[1,1024]{1,0:T(1,128)}, f32[1,1024]{1,0:T(1,128)S(1)}, u32[]{:S(2)}) copy-start(f32[1,1024]{1,0:T(1,128)S(1)} %get-tuple-element.154) | copy-start | bytes 12292
  71.1 204.1 %copy-start.70 = (f32[1,1024]{1,0:T(1,128)}, f32[1,1024]{1,0:T(1,128)S(1)}, u32[]{:S(2)}) copy-start(f32[1,1024]{1,0:T(1,128)S(1)} %get-tuple-element.155) | copy-start | bytes 12292
  71.1 204.1 %copy-start.72 = (f32[1,1024]{1,0:T(1,128)}, f32[1,1024]{1,0:T(1,128)S(1)}, u32[]{:S(2)}) copy-start(f32[1,1024]{1,0:T(1,128)S(1)} %get-tuple-element.156) | copy-start | bytes 12292
  71.1 204.1 %copy-start.74 = (f32[1,1024]{1,0:T(1,128)}, f32[1,1024]{1,0:T(1,128)S(1)}, u32[]{:S(2)}) copy-start(f32[1,1024]{1,0:T(1,128)S(1)} %get-tuple-element.157) | copy-start | bytes 12292
  71.1 204.1 %copy-start.76 = (f32[1,1024]{1,0:T(1,128)}, f32[1,1024]{1,0:T(1,128)S(1)}, u32[]{:S(2)}) copy-start(f32[1,1024]{1,0:T(1,128)S(1)} %get-tuple-element.158) | copy-start | bytes 12292
  71.2 204.1 %copy-start.78 = (f32[1,1024]{1,0:T(1,128)}, f32[1,1024]{1,0:T(1,128)S(1)}, u32[]{:S(2)}) copy-start(f32[1,1024]{1,0:T(1,128)S(1)} %get-tuple-element.159) | copy-start | bytes 12292
  254.1 5.2 collective-permute-start.4
  255.5 5.2 collective-permute-start.1
  257.9 10.1 collective-permute-start.6
  851.9 815.9 %copy-start.81 = (f32[1024]{0:T(1024)S(1)}, f32[1024]{0:T(1024)}, u32[]{:S(2)}) copy-start(f32[1024]{0:T(1024)} %get-tuple-element.85) | copy-start | bytes 12292
  851.9 815.9 %copy-start.82 = (f32[1024]{0:T(1024)S(1)}, f32[1024]{0:T(1024)}, u32[]{:S(2)}) copy-start(f32[1024]{0:T(1024)} %get-tuple-element.86) | copy-start | bytes 12292
  1687.3 89.6 %collective-permute-start.10 = (bf16[1,3,3,1024]{3,2,1,0:T(4,128)(2,1)S(1)}, bf16[1,3,3,1024]{3,2,1,0:T(4,128)(2,1)S(1)}, u32[]{:S(2)}, u32[]{:S(2)}) collective-permute-start(bf16[1,3,3,1024]{3,2,1,0:T(4,128)(2,1)S(1)} %get-tuple-element.97), channel_id=1, source_target_pairs={{3,0},{4,1},{5,2},{6,3},{7,4},{8,5},{9,6},{10,7},{11,8},{12,9},{13... | collective-permute-start | bytes 55304 | tf_op jit(solution)/shard_map/ppermute | solution.py:15
  1761.7 16.6 collective-permute-start.13
  1763.0 16.6 collective-permute-start.15
  1772.5 14.5 collective-permute-start.12
  1773.8 13.3 collective-permute-start.8
  1776.9 10.2 collective-permute-start.9
  1778.2 12.2 collective-permute-start.11
  1779.6 10.9 collective-permute-start.14
  (79 other events, 7042.1 us)
Sparse Core Ops, SparseCore 0:
  10.2 825.4 all-gather.5
  838.0 818.7 all-gather.7
  1777.0 86.5 reduce-scatter.3
where the time goes:
time: 2040 us
  waiting for transfers between devices  1440 us (71%)
  blocking collectives  460 us (23%)
  starting transfers between devices  48 us (2%)
  local copies, waits for them, and re-layouts  30.7 us (2%)
  other arithmetic  22.4 us (1%)
    all_gather x1, waiting for transfers between devices, per_device(): rows_out = lax.all_gather(out_weight, ('dp', 'tile'), axis=0, tiled=True)  805 us
    all_gather x1, waiting for transfers between devices, per_device(): rows_in = lax.all_gather(in_weight, ('dp', 'tile'), axis=0, tiled=True)  558 us
    unnamed x3, blocking collectives  252 us
    psum x1, blocking collectives, per_device(): lax.psum((shared[0], shared[1], shared[2], shared[3], shared[4]), 'tile')  167 us
    unnamed x4, waiting for transfers between devices  68 us
    ppermute x16, starting transfers between devices, passed_along(): return lax.ppermute(block, axis, route)  47.9 us
    all_gather x1, blocking collectives, per_device(): lax.all_gather(kernel, 'dp', axis=1, tiled=True)  40.8 us
  transfers between devices with their start and end apart: 19, of which 6 were waited for; matrix products, arithmetic and copies ran while one was open for 2% of the time, Pallas kernels for 0%

commit v1 on v0

v1 whole, which is shorter than its diff:
```python
import functools
import math

import jax
import jax.numpy as jnp
from jax import lax
from jax.experimental import pallas as pl
from jax.experimental.pallas import tpu as pltpu
from jax.sharding import PartitionSpec as P

KS = 7
GX = 4
NX, NY, NZ = 4, 8, 8
MESH = pl.DeviceIdType.MESH
VMEM = pl.BlockSpec(memory_space=pltpu.VMEM)
F32 = jnp.float32
BF16 = jnp.bfloat16
DMA = pltpu.SemaphoreType.DMA


def place():
    dp = lax.axis_index("dp")
    tile = lax.axis_index("tile")
    x = lax.rem(dp, 4)
    y = lax.div(tile, 16) * 4 + lax.div(dp, 4)
    z = lax.rem(lax.div(tile, 2), 8)
    core = lax.rem(tile, 2)
    return x, y, z, core


def device(x, y, z, core):
    return (lax.rem(y, 4) * 4 + x, lax.div(y, 4) * 16 + z * 2 + core)


def turned(index, by, size):
    return lax.rem(index + (by % size), size)


def greet(barrier, peer):
    pl.semaphore_signal(barrier, inc=1, device_id=peer, device_id_type=MESH)


def remote(src, dst, ssem, rsem, peer):
    return pltpu.make_async_remote_copy(
        src_ref=src, dst_ref=dst, send_sem=ssem, recv_sem=rsem, device_id=peer, device_id_type=MESH
    )


STEPS = [(-1, 0), (1, 0), (0, -1), (0, 1), (-1, -1), (-1, 1), (1, -1), (1, 1)]


def halo_sides():
    dp = lax.axis_index("dp")
    tile = lax.axis_index("tile")
    ty = lax.div(tile, GX)
    tx = lax.rem(tile, GX)
    sides = []
    for dr, dc in STEPS:
        there = None
        for ok in ([ty >= 1] if dr < 0 else [ty <= 6] if dr > 0 else []) + (
            [tx >= 1] if dc < 0 else [tx <= 2] if dc > 0 else []
        ):
            there = ok if there is None else there & ok
        sides.append((there, (dp, tile + dr * GX + dc)))
    return sides


def halo_greet(barrier):
    for there, peer in halo_sides():
        @pl.when(there)
        def _():
            greet(barrier, peer)


def halo_count():
    count = 0
    for there, _ in halo_sides():
        count = count + there.astype(jnp.int32)
    return count


def halo_copies(field, edges, rows, cols, cors, ssem, rsem):
    src = [field.at[0:3], field.at[5:8], edges.at[0:24], edges.at[24:48]]
    src += [edges.at[48 + 16 * k : 64 + 16 * k] for k in range(4)]
    dst = [rows.at[1], rows.at[0], cols.at[1], cols.at[0], cors.at[3], cors.at[2], cors.at[1], cors.at[0]]
    back = [1, 0, 3, 2, 7, 6, 5, 4]
    out = []
    for k, (there, peer) in enumerate(halo_sides()):
        out.append((there, remote(src[k], dst[k], ssem.at[k], rsem.at[back[k]], peer)))
    return out, dst, back


def halo_start(copies):
    for there, copy in copies[0]:
        @pl.when(there)
        def _():
            copy.start()


def halo_finish(copies, rsem):
    moves, dst, back = copies
    for k, (there, copy) in enumerate(moves):
        landed = dst[back[k]]
        @pl.when(there)
        def _():
            pltpu.make_async_copy(landed, landed, rsem.at[k]).wait()
            copy.wait_send()

        @pl.when(jnp.logical_not(there))
        def _():
            landed[...] = jnp.zeros(landed.shape, landed.dtype)


def head_body(field, edges, par, bia, rows, cols, cors, pars, bias, row, zbias, hs, hr, ps, pr, zs, zr, bs, br):
    x, y, z, core = place()
    dp = lax.axis_index("dp")
    tile = lax.axis_index("tile")
    barrier = pltpu.get_barrier_semaphore()
    halo_greet(barrier)
    dps = [(turned(dp, k, 16), tile) for k in range(1, 16)]
    zps = [device(x, y, turned(z, k, NZ), core) for k in range(1, NZ)]
    xys = []
    for k in range(1, 32):
        ky, kx = k // 4, k % 4
        xys.append(device(turned(x, kx, NX), turned(y, ky, NY), z, core))
    for peer in dps + zps + xys:
        greet(barrier, peer)
    pl.semaphore_wait(barrier, 15 + 7 + 31 + halo_count())
    zcp = [remote(bia, zbias.at[z], zs.at[k], zr.at[k], peer) for k, peer in enumerate(zps)]
    for copy in zcp:
        copy.start()
    copies = halo_copies(field, edges, rows, cols, cors, hs, hr)
    halo_start(copies)
    pcp = [remote(par, pars.at[dp], ps.at[k], pr.at[k], peer) for k, peer in enumerate(dps)]
    for copy in pcp:
        copy.start()
    zbias[z] = bia[...]
    pars[dp] = par[...]
    for copy in zcp:
        copy.wait()
    total = zbias[0]
    for k in range(1, NZ):
        total = total + pltpu.roll(zbias[k], 6 * k, 1)
    row[...] = total
    me = x * 8 + y
    bias[me] = total
    bcp = [remote(row, bias.at[me], bs.at[k], br.at[k], peer) for k, peer in enumerate(xys)]
    for copy in bcp:
        copy.start()
    halo_finish(copies, hr)
    for copy in pcp:
        copy.wait()
    for copy in bcp:
        copy.wait()


def head(field, edges, par, bia):
    width = field.shape[-1]
    return pl.pallas_call(
        head_body,
        out_shape=(
            jax.ShapeDtypeStruct((2, 3, 16, width), BF16),
            jax.ShapeDtypeStruct((2, 24, width), BF16),
            jax.ShapeDtypeStruct((4, 16, width), BF16),
            jax.ShapeDtypeStruct((16, 28, 128), F32),
            jax.ShapeDtypeStruct((32, 1, 128), F32),
        ),
        in_specs=[VMEM] * 4,
        out_specs=[VMEM] * 5,
        scratch_shapes=[
            pltpu.VMEM((1, 128), F32),
            pltpu.VMEM((8, 1, 128), F32),
            DMA((8,)), DMA((8,)), DMA((15,)), DMA((15,)), DMA((7,)), DMA((7,)), DMA((31,)), DMA((31,)),
        ],
        compiler_params=pltpu.CompilerParams(collective_id=0, has_side_effects=True),
        name="head",
    )(field, edges, par, bia)


def halo_body(field, edges, rows, cols, cors, hs, hr):
    barrier = pltpu.get_barrier_semaphore()
    halo_greet(barrier)
    pl.semaphore_wait(barrier, halo_count())
    copies = halo_copies(field, edges, rows, cols, cors, hs, hr)
    halo_start(copies)
    halo_finish(copies, hr)


def halo(field, edges):
    width = field.shape[-1]
    return pl.pallas_call(
        halo_body,
        out_shape=(
            jax.ShapeDtypeStruct((2, 3, 16, width), BF16),
            jax.ShapeDtypeStruct((2, 24, width), BF16),
            jax.ShapeDtypeStruct((4, 16, width), BF16),
        ),
        in_specs=[VMEM] * 2,
        out_specs=[VMEM] * 3,
        scratch_shapes=[DMA((8,)), DMA((8,))],
        compiler_params=pltpu.CompilerParams(collective_id=1, has_side_effects=True),
        name="halo",
    )(field, edges)


def edges_of(field):
    width = field.shape[-1]

    def corner(rows, cols):
        return jnp.pad(field[rows, cols].reshape(9, width), ((0, 7), (0, 0)))

    low, high, left, right = slice(0, 3), slice(5, 8), slice(0, 3), slice(13, 16)
    return jnp.concatenate(
        [
            field[:, left].reshape(24, width),
            field[:, right].reshape(24, width),
            corner(low, left),
            corner(low, right),
            corner(high, left),
            corner(high, right),
        ]
    )


def padded_of(field, rows, cols, cors):
    width = field.shape[-1]
    cor = cors[:, :9].reshape(4, 3, 3, width)
    side = cols.reshape(2, 8, 3, width)
    return jnp.concatenate(
        [
            jnp.concatenate([cor[0], rows[0], cor[1]], axis=1),
            jnp.concatenate([side[0], field, side[1]], axis=1),
            jnp.concatenate([cor[2], rows[1], cor[3]], axis=1),
        ]
    )


OFF4 = [0, -1, 1, 2]
OFF8 = [0, -1, 1, -2, 2, -3, 3, 4]


def ring_slots(n, count):
    half = n // 2
    right = [(s, j) for s in range(1, half) for j in range(count)] + [(half, j) for j in range(count // 2)]
    left = [(s, j) for s in range(1, half) for j in range(count)] + [(half, j) for j in range(count // 2, count)]
    return right, left


class Ring:
    def __init__(self, n, count, offs, sub, peers, ssem, rsem, wire):
        self.n, self.count, self.offs, self.sub, self.peers = n, count, offs, sub, peers
        self.ssem, self.rsem, self.wire = ssem, rsem, wire
        self.slots = ring_slots(n, count)

    def copy(self, way, s, j):
        i = self.slots[way].index((s, j))
        ref = self.sub(-(s - 1) if way == 0 else (s - 1), j)
        return remote(ref, ref, self.ssem.at[way, i], self.rsem.at[way, i], self.peers[way])

    def landed(self, way, s, j):
        i = self.slots[way].index((s, j))
        ref = self.sub(-s if way == 0 else s, j)
        return pltpu.make_async_copy(ref, ref, self.rsem.at[way, i])


def plan(outer, inner):
    events = []
    latency = 1.7
    for c, (o, i) in enumerate(zip(outer, inner)):
        ready = {0: 0.0}
        for way in (0, 1):
            t, got = 0.0, {}
            for s, j in i.slots[way]:
                t = max(t, 0.0 if s == 1 else got[s - 1, j]) + i.wire
                got[s, j] = t + latency
                events.append((got[s, j], c, 0, way, s, j))
        for way in (0, 1):
            for s, j in i.slots[way]:
                pass
        half = i.n // 2
        seen = {(e[3], e[4], e[5]): e[0] for e in events if e[1] == c and e[2] == 0}
        for k, off in enumerate(o.offs):
            if off == 0:
                continue
            if abs(off) == half:
                ready[k] = max(v for (w, s, j), v in seen.items() if s == half)
            else:
                ready[k] = max(v for (w, s, j), v in seen.items() if s == abs(off) and w == (0 if off < 0 else 1))
        for way in (0, 1):
            t, got = 0.0, {}
            for s, j in o.slots[way]:
                t = max(t, ready[j] if s == 1 else got[s - 1, j]) + o.wire
                got[s, j] = t + latency
                events.append((got[s, j], c, 1, way, s, j))
    return sorted(events)


def mlp_body(normed, bout, wt, bias, mlp_out, bn_out, rz, ry, scr, g0, g1, g2, act, acc, part,
             as_, ar, s0s, s0r, p1s, p1r, q0s, q0r, q1s, q1r, q2s, q2r, r0s, r0r, r1s, r1r, r2s, r2r, es, er):
    x, y, z, core = place()
    barrier = pltpu.get_barrier_semaphore()
    sibling = device(x, y, z, 1 - core)
    xps = [device(turned(x, k, NX), y, z, core) for k in range(1, NX)]
    yps = [device(x, turned(y, k, NY), z, core) for k in range(1, NY)]
    zps = [device(x, y, turned(z, k, NZ), core) for k in range(1, NZ)]
    for peer in [sibling] + xps + yps + zps:
        greet(barrier, peer)
    pl.semaphore_wait(barrier, 1 + 3 + 7 + 7)

    copies = []
    for k in range(1, NZ):
        copies.append(remote(wt.at[turned(z, k, NZ)], rz.at[z], s0s.at[0, k - 1], s0r.at[0, k - 1], zps[k - 1]))
    for k in range(1, NY):
        copies.append(remote(wt.at[turned(y, k, NY)], ry.at[y], s0s.at[1, k - 1], s0r.at[1, k - 1], yps[k - 1]))
    for copy in copies:
        copy.start()
    ship = []
    for a, src in enumerate((normed, bout)):
        ship.append(remote(src, act.at[a, core], as_.at[a], ar.at[a], sibling))
        ship[-1].start()
    rz[z] = wt[z]
    ry[y] = wt[y]
    act[0, core] = normed[...]
    act[1, core] = bout[...]
    for copy in copies:
        copy.wait()
    home = (g0.at[y, x, z], g1.at[x, z, y], g2.at[z, y, x])
    for k in range(3):
        src = (rz, ry, ry)[k]
        for d in range(8):
            val = src[d].astype(F32)
            scr[k, 0, 2 * d : 2 * d + 2, :] = val[2 * k : 2 * k + 2]
            scr[k, 1, 2 * d : 2 * d + 2, :] = val[6 + 2 * k : 8 + 2 * k]
        home[k][...] = scr[k].astype(BF16)
    first = []
    for k, peers in enumerate((zps, yps, xps)):
        row = [remote(home[k], home[k], p1s.at[k, i], p1r.at[k, i], peer) for i, peer in enumerate(peers)]
        for copy in row:
            copy.start()
        first.append(row)

    xr, xl = xps[0], xps[-1]
    yr, yl = yps[0], yps[-1]
    zr, zl = zps[0], zps[-1]
    inner = [
        Ring(4, 2, None, lambda b, j: g0.at[y, turned(x, b, 4), pl.ds(4 * j, 4)], (xr, xl), q0s, q0r, 0.7),
        Ring(8, 2, None, lambda b, j: g1.at[x, turned(z, b, 8), pl.ds(4 * j, 4)], (zr, zl), q1s, q1r, 0.7),
        Ring(8, 2, None, lambda b, j: g2.at[z, turned(y, b, 8), pl.ds(2 * j, 2)], (yr, yl), q2s, q2r, 0.35),
    ]
    outer = [
        Ring(8, 4, OFF4, lambda b, j: g0.at[turned(y, b, 8), turned(x, OFF4[j], 4)], (yr, yl), r0s, r0r, 1.4),
        Ring(4, 8, OFF8, lambda b, j: g1.at[turned(x, b, 4), turned(z, OFF8[j], 8)], (xr, xl), r1s, r1r, 1.4),
        Ring(8, 8, OFF8, lambda b, j: g2.at[turned(z, b, 8), turned(y, OFF8[j], 8)], (zr, zl), r2s, r2r, 0.7),
    ]
    started = []

    def go(copy):
        copy.start()
        started.append(copy)

    for k in range(3):
        for copy in first[k]:
            copy.wait()
        for way in (0, 1):
            go(outer[k].copy(way, 1, 0)) if (1, 0) in outer[k].slots[way] else None
            for j in range(2):
                go(inner[k].copy(way, 1, j))
    for _, k, level, way, s, j in plan(outer, inner):
        ring = (inner, outer)[level][k]
        ring.landed(way, s, j).wait()
        if (s + 1, j) in ring.slots[way]:
            go(ring.copy(way, s + 1, j))
        if level == 0 and j == (1 if s < ring.n // 2 else way):
            half = ring.n // 2
            if s == half:
                if way == 0:
                    continue
                index = outer[k].offs.index(half)
            else:
                index = outer[k].offs.index(-s if way == 0 else s)
            for w in (0, 1):
                if (1, index) in outer[k].slots[w]:
                    go(outer[k].copy(w, 1, index))
    for copy in ship:
        copy.wait()

    acc[...] = jnp.zeros_like(acc)
    a_in = act[0].reshape(256, 1024)
    a_out = act[1].reshape(256, 1024)
    nt = (((1,), (1,)), ((), ()))

    def chunk(read, number):
        w_in = jnp.concatenate([read(cb, 0).reshape(256, 128) for cb in range(8)], axis=1)
        w_out = jnp.concatenate([read(cb, 1).reshape(256, 128) for cb in range(8)], axis=1)
        pre = lax.dot_general(a_in, w_in, nt, preferred_element_type=F32) + bias[number]
        back = lax.dot_general(a_out, w_out, nt, preferred_element_type=F32)
        cdf = 0.5 * (1.0 + lax.erf(pre * 0.7071067811865476))
        hidden = (pre * cdf).astype(BF16)
        slope = cdf + pre * jnp.exp(-0.5 * pre * pre) * 0.3989422804014327
        back_pre = (back * slope).astype(BF16)
        acc[0] += jnp.dot(hidden, w_out, preferred_element_type=F32).reshape(2, 128, 1024)
        acc[1] += jnp.dot(back_pre, w_in, preferred_element_type=F32).reshape(2, 128, 1024)

    for k in range(3):
        def step(i, carry):
            if k == 0:
                chunk(lambda cb, m: g0[pl.ds(4 * i, 4), :, cb, m], i)
            elif k == 1:
                chunk(lambda cb, m: g1[pl.ds(2 * i, 2), :, cb, m], 2 + i)
            else:
                chunk(lambda cb, m: g2[pl.ds(4 * i, 4), cb, :, m], 4 + i)
            return carry

        lax.fori_loop(0, 2, step, 0)
    swap = []
    for a in range(2):
        swap.append(remote(acc.at[a, 1 - core], part.at[a], es.at[a], er.at[a], sibling))
        swap[-1].start()
    for a, out in enumerate((mlp_out, bn_out)):
        swap[a].wait_recv()
        out[...] = acc[a, core] + part[a]
    for copy in started + swap:
        copy.wait_send()


def mlp(normed, bout, wt, bias):
    tile = (2, 16, 128)
    return pl.pallas_call(
        mlp_body,
        out_shape=(jax.ShapeDtypeStruct((128, 1024), F32), jax.ShapeDtypeStruct((128, 1024), F32)),
        in_specs=[VMEM] * 4,
        out_specs=[VMEM] * 2,
        scratch_shapes=[
            pltpu.VMEM((8, 16, 128), BF16),
            pltpu.VMEM((8, 16, 128), BF16),
            pltpu.VMEM((3, 2, 16, 128), F32),
            pltpu.VMEM((8, 4, 8) + tile, BF16),
            pltpu.VMEM((4, 8, 8) + tile, BF16),
            pltpu.VMEM((8, 8, 4) + tile, BF16),
            pltpu.VMEM((2, 2, 128, 1024), BF16),
            pltpu.VMEM((2, 2, 128, 1024), F32),
            pltpu.VMEM((2, 128, 1024), F32),
            DMA((2,)), DMA((2,)), DMA((2, 7)), DMA((2, 7)), DMA((3, 7)), DMA((3, 7)),
            DMA((2, 3)), DMA((2, 3)), DMA((2, 7)), DMA((2, 7)), DMA((2, 7)), DMA((2, 7)),
            DMA((2, 14)), DMA((2, 14)), DMA((2, 12)), DMA((2, 12)), DMA((2, 28)), DMA((2, 28)),
            DMA((2,)), DMA((2,)),
        ],
        compiler_params=pltpu.CompilerParams(
            collective_id=2, has_side_effects=True, vmem_limit_bytes=48 * 1024 * 1024
        ),
        name="mlp",
    )(normed, bout, wt, bias)


def reduce_body(sums, out, r1, r2, r3, mid, low, fin, s1, t1, s2, t2, s3, t3, s4, t4):
    x, y, z, core = place()
    yl, yh = lax.rem(y, 4), lax.div(y, 4)
    xl, xh = lax.rem(x, 2), lax.div(x, 2)
    mine = yl * 2 + xh
    barrier = pltpu.get_barrier_semaphore()
    firsts, blocks = [], []
    for k in range(1, 8):
        other = turned(mine, k, 8)
        blocks.append(other)
        firsts.append(device(lax.rem(other, 2) * 2 + xl, yh * 4 + lax.div(other, 2), z, core))
    zps = [device(x, y, turned(z, k, NZ), core) for k in range(1, NZ)]
    member = yh * 4 + xl * 2 + core
    thirds = []
    for k in range(1, 8):
        o = turned(member, k, 8)
        thirds.append(device(xh * 2 + lax.rem(lax.div(o, 2), 2), lax.div(o, 4) * 4 + yl, z, lax.rem(o, 2)))
    for peer in firsts + zps + thirds:
        greet(barrier, peer)
    pl.semaphore_wait(barrier, 21)

    def lanes(block):
        return sums.at[:, pl.ds(pl.multiple_of(block * 128, 128), 128)]

    c1 = [remote(lanes(blocks[k]), r1.at[mine], s1.at[k], t1.at[k], firsts[k]) for k in range(7)]
    for copy in c1:
        copy.start()
    r1[mine] = lanes(mine)[...]
    for copy in c1:
        copy.wait()
    mid[...] = jnp.sum(r1[...], axis=0).reshape(8, 8, 128)
    c2 = [remote(mid.at[turned(z, k + 1, 8)], r2.at[z], s2.at[k], t2.at[k], zps[k]) for k in range(7)]
    for copy in c2:
        copy.start()
    r2[z] = mid[z]
    for copy in c2:
        copy.wait()
    low[...] = jnp.sum(r2[...], axis=0)
    c3 = [remote(low, r3.at[member], s3.at[k], t3.at[k], thirds[k]) for k in range(7)]
    for copy in c3:
        copy.start()
    r3[member] = low[...]
    for copy in c3:
        copy.wait()
    fin[...] = jnp.sum(r3[...], axis=0)
    c4 = [remote(fin, out.at[z], s4.at[k], t4.at[k], zps[k]) for k in range(7)]
    for copy in c4:
        copy.start()
    out[z] = fin[...]
    for copy in c4:
        copy.wait()


def reduced(sums):
    return pl.pallas_call(
        reduce_body,
        out_shape=jax.ShapeDtypeStruct((8, 8, 128), F32),
        in_specs=[VMEM],
        out_specs=VMEM,
        scratch_shapes=[
            pltpu.VMEM((8, 64, 128), F32),
            pltpu.VMEM((8, 8, 128), F32),
            pltpu.VMEM((8, 8, 128), F32),
            pltpu.VMEM((8, 8, 128), F32),
            pltpu.VMEM((8, 128), F32),
            pltpu.VMEM((8, 128), F32),
        ]
        + [DMA((7,))] * 8,
        compiler_params=pltpu.CompilerParams(collective_id=3, has_side_effects=True),
        name="reduced",
    )(sums)


def per_device(
    features,
    cotangent,
    in_weight,
    out_weight,
    hidden_bias,
    kernel,
    conv_bias,
    norm_gain,
    norm_bias,
    layer_scale,
    out_bias,
):
    _, _, rows, cols, width = features.shape
    margin = KS // 2
    pixel_rows = rows * cols
    field = features.reshape(rows, cols, width)
    slab = jnp.concatenate(
        [kernel] + [v[None] for v in (conv_bias, norm_gain, norm_bias, layer_scale, out_bias)] + [jnp.zeros((2, 64), F32)]
    )
    par = jnp.concatenate([slab[:28], slab[28:]], axis=1)
    bia = jnp.pad(hidden_bias.astype(F32)[None], ((0, 0), (0, 122)))
    hrows, hcols, hcors, pars, bias = head(field, edges_of(field), par, bia)
    pars = pars.reshape(16, 28, 2, 64).transpose(2, 1, 0, 3).reshape(56, width)
    kernel_all = pars[:49]
    cbias, gain, nbias, lscale, obias = (pars[49 + i] for i in range(5))
    b = bias.reshape(4, 8, 128)[:, :, :48].reshape(4, 8, 8, 6)
    bias_rows = jnp.concatenate(
        [
            b[..., 0:2].transpose(1, 0, 2, 3).reshape(2, 1, 256),
            b[..., 2:4].transpose(0, 2, 1, 3).reshape(2, 1, 256),
            b[..., 4:6].transpose(2, 0, 1, 3).reshape(2, 1, 256),
        ]
    )
    both = jnp.concatenate([in_weight, out_weight, jnp.zeros((4, width), BF16)])
    wt = both.reshape(16, 8, 128).transpose(1, 0, 2)

    padded = padded_of(field, hrows, hcols, hcors)
    convolved = jnp.zeros((rows, cols, width), F32) + cbias
    for tap_row in range(KS):
        for tap_col in range(KS):
            window = padded[tap_row : tap_row + rows, tap_col : tap_col + cols, :].astype(F32)
            convolved = convolved + kernel_all[tap_row * KS + tap_col] * window
    average = jnp.mean(convolved, axis=-1, keepdims=True)
    centered = convolved - average
    variance = jnp.mean(centered * centered, axis=-1, keepdims=True)
    inverse = lax.rsqrt(variance + 1e-06)
    standard = (centered * inverse).reshape(pixel_rows, width)
    inverse = inverse.reshape(pixel_rows, 1)
    normed = (standard * gain + nbias).astype(BF16)
    upstream = cotangent.reshape(pixel_rows, width).astype(F32)
    back_out = (upstream * lscale).astype(BF16)

    mlp_sum, back_normed = mlp(normed, back_out, wt, bias_rows)

    projected = mlp_sum + obias
    source = field.reshape(pixel_rows, width).astype(F32)
    block_out = (source + lscale * projected).astype(BF16).reshape(features.shape)
    scale_part = jnp.sum(upstream * projected, axis=0)
    gain_part = jnp.sum(back_normed * standard, axis=0)
    nbias_part = jnp.sum(back_normed, axis=0)
    scaled = back_normed * gain
    back_conv = inverse * (
        scaled
        - jnp.mean(scaled, axis=-1, keepdims=True)
        - standard * jnp.mean(scaled * standard, axis=-1, keepdims=True)
    )
    cbias_part = jnp.sum(back_conv, axis=0)
    back_grid = back_conv.reshape(rows, cols, width)
    wire = back_grid.astype(BF16)
    wrows, wcols, wcors = halo(wire, edges_of(wire))
    back_padded = padded_of(wire, wrows, wcols, wcors)
    grad_grid = upstream.reshape(rows, cols, width)
    kernel_rows = []
    for tap_row in range(KS):
        for tap_col in range(KS):
            tap_weight = kernel_all[tap_row * KS + tap_col]
            flipped = back_padded[
                2 * margin - tap_row : 2 * margin - tap_row + rows,
                2 * margin - tap_col : 2 * margin - tap_col + cols,
                :,
            ].astype(F32)
            grad_grid = grad_grid + tap_weight * flipped
            window = padded[tap_row : tap_row + rows, tap_col : tap_col + cols, :].astype(F32)
            kernel_rows.append(jnp.sum(back_grid * window, axis=(0, 1)))
    grad_input = grad_grid.astype(BF16).reshape(features.shape)
    sums = jnp.stack(kernel_rows + [cbias_part, gain_part, nbias_part, scale_part] + [jnp.zeros(width, F32)] * 11)
    total = reduced(sums).reshape(64, 2, 64)
    half = lax.rem(lax.axis_index("dp"), 2)
    factor = 1.0 / math.sqrt(65536)
    total = jnp.where(half == 0, total[:, 0], total[:, 1]) * factor
    return (block_out, grad_input, total[:49], total[49], total[50], total[51], total[52])


def solution(mesh):
    placed = (
        P("dp", "tile", None, None, None),
        P("dp", "tile", None, None, None),
        P(("dp", "tile"), None),
        P(("dp", "tile"), None),
        P(("dp", "tile")),
        P(None, "dp"),
        P("dp"),
        P("dp"),
        P("dp"),
        P("dp"),
        P("dp"),
    )
    return jax.shard_map(
        per_device,
        mesh=mesh,
        in_specs=placed,
        out_specs=(
            P("dp", "tile", None, None, None),
            P("dp", "tile", None, None, None),
            P(None, "dp"),
            P("dp"),
            P("dp"),
            P("dp"),
            P("dp"),
        ),
        check_vma=False,
    )
```

time: 2040 us -> 183 us (0.09)
  the two profiles are of different devices: /device:TPU:2 before, /device:TPU:40 now
where the time goes in v1:
time: 183 us; the launch traced here: 182 us
  Pallas kernels  137 us (75%)
  other arithmetic  21.9 us (12%)
  local copies, waits for them, and re-layouts  20.2 us (11%)
  between operations  2.85 us (2%)
    pallas_call x1, Pallas kernels, mlp(): pl.pallas_call(mlp_body, out_shape=(jax.ShapeDtypeStruct((128, 1024), F32...  56 us
    pallas_call x1, Pallas kernels, head(): pl.pallas_call(head_body, out_shape=(jax.ShapeDtypeStruct((2, 3, 16, widt...  30.7 us
    pallas_call x1, Pallas kernels, reduced(): pl.pallas_call(reduce_body, out_shape=jax.ShapeDtypeStruct((8, 8, 128), F...  29.5 us
    pallas_call x1, Pallas kernels, halo(): pl.pallas_call(halo_body, out_shape=(jax.ShapeDtypeStruct((2, 3, 16, widt...  20.9 us
    reduce_sum x1, other arithmetic, per_device(): average = jnp.mean(convolved, axis=-1, keepdims=True)  5.83 us
    another operation x4, local copies, waits for them, and re-layouts, per_device(): jnp.stack(kernel_rows + [cbias_part, gain_part, nbias_part, scale_part] +...  5.28 us
    reshape x1, other arithmetic, per_device(): grad_input = grad_grid.astype(BF16).reshape(features.shape)  4.82 us
    reduce_sum x3, other arithmetic, per_device(): kernel_rows.append(jnp.sum(back_grid * window, axis=(0, 1)))  4.8 us

profile of v1, /device:TPU:40, one launch (start us, length us, event | category | flops | bytes accessed | tf_op | source)
XLA Modules:
  0.0 182.0 jit_solution(3191328433894043058)
XLA Ops:
  0.6 1.0 fusion.148
  1.9 0.9 fusion.147
  3.1 0.7 pad_maximum_fusion.4.par
  3.8 0.5 pad_convert_fusion.bia
  4.3 30.7 %head.1 = (bf16[2,3,16,1024]{3,2,1,0:T(8,128)(2,1)}, bf16[2,24,1024]{2,1,0:T(8,128)(2,1)}, bf16[4,16,1024]{2,1,0:T(8,128)(2,1)}, f32[16,28,128]{2,1,0:T(8,128)}, f32[32,1,128]{2,1,0:T(1,128)}) custom-call(bf16[8,16,1024]{2,1,0:T(8,128)(2,1)} %bitcast.300, bf16[112,1024]{1,0:T(8,128)(2,1)} %copy-done.7, f32[28,128]{1,0:T(8,128)} %pad_maximum_fusion.4.par, ...), custom_call_target="tpu_custom_call" | custom-call | tf_op jit(solution)/shard_map/head/pallas_call | solution.py:159
  35.0 0.9 fusion.155
  36.0 0.8 fusion.153
  37.4 0.6 copy-done.9
  38.6 0.6 fusion.150
  39.3 0.6 fusion.149
  40.3 5.8 %fusion.143 = (f32[8,16]{1,0:T(8,128)S(1)}, f32[8,16,1024]{2,1,0:T(8,128)S(1)}) fusion(bf16[11,22,1024]{2,1,0:T(8,128)(2,1)S(1)} %get-tuple-element.101, f32[1024]{0:T(1024)S(1)} %bitcast.347, f32[1024]{0:T(1024)S(1)} %bitcast.349, f32[1024]{0:T(1024)S(1)} %bitcast.351, f32[1024]{0:T(1024)S(1)} %bitcast.353, f32[1024]{0:T(1024)S(1)} %bitcast.355, ...), kind=kLoop, calls=%fused_computation.309 | loop fusion | flops 21757824 | bytes 12100096 | tf_op jit(solution)/shard_map/reduce_sum | solution.py:571
  46.8 0.8 copy-done.3
  47.6 0.8 fusion.124
  49.5 56.0 %mlp.1 = (f32[128,1024]{1,0:T(8,128)S(1)}, f32[128,1024]{1,0:T(8,128)S(1)}) custom-call(bf16[128,1024]{1,0:T(8,128)(2,1)S(1)} %get-tuple-element.196.normed, bf16[128,1024]{1,0:T(8,128)(2,1)S(1)} %get-tuple-element.195.bout, bf16[8,16,128]{2,1,0:T(8,128)(2,1)S(1)} %bitcast_bitcast_fusion.wt, f32[6,1,256]{2,1,0:T(1,128)S(1)} %pad_maximum_fusion.5.bias), custom_call_target="tpu_custom_call" | custom-call | tf_op jit(solution)/shard_map/mlp/pallas_call | solution.py:428
  105.5 0.8 fusion.131
  106.3 0.5 broadcast_multiply_fusion.1
  106.8 0.5 broadcast_multiply_fusion.2
  107.3 0.6 rsqrt.16
  107.9 2.7 %fusion.96 = (f32[1024]{0:T(1024)}, f32[1024]{0:T(1024)}, f32[1024]{0:T(1024)}, f32[1024]{0:T(1024)}, f32[1024]{0:T(1024)}, /*index=5*/f32[1024]{0:T(1024)}, f32...) fusion(bf16[11,22,1024]{2,1,0:T(8,128)(2,1)S(1)} %get-tuple-ele, ...), kind=kLoop, calls=%fused_computation.198 | loop fusion | flops 7714816 | bytes 6370816 | tf_op jit(solution)/shard_map/reduce_sum | solution.py:612
  110.6 1.0 fusion.45
  111.6 1.1 fusion.78
  113.0 1.6 fusion.125
  114.7 5.3 %stack.223.sums = f32[64,1024]{1,0:T(8,128)} concatenate(f32[1,1024]{1,0:T(1,128)S(1)} %bitcast.433, f32[1,1024]{1,0:T(1,128)S(1)} %bitcast.434, f32[1,1024]{1,0:T(1,128)S(1)} %bitcast.435, f32[1,1024]{1,0:T(1,128)S(1)} %bitcast.465, f32[1,1024]{1,0:T(1,128)S(1)} %bitcast.464, f32[1,1024]{1,0:T(1,128)S(1)} %bitcast.463, f32[1,1024]{1,0:T(1,128)S(1)} %bitcast.462, ...), dimensions={0} | concatenate | bytes 524288 | tf_op jit(solution)/shard_map/stack | solution.py:614
  120.0 29.5 %reduced.1 = f32[8,8,128]{2,1,0:T(8,128)} custom-call(f32[64,1024]{1,0:T(8,128)} %stack.223.sums), custom_call_target="tpu_custom_call" | custom-call | tf_op jit(solution)/shard_map/reduced/pallas_call | solution.py:509
  149.5 0.9 reshape.251
  150.4 0.6 slice_bitcast_fusion.7
  151.0 0.5 slice_bitcast_fusion.8
  152.4 0.7 copy-done.8
  153.1 20.9 %halo.1 = (bf16[2,3,16,1024]{3,2,1,0:T(8,128)(2,1)}, bf16[2,24,1024]{2,1,0:T(8,128)(2,1)}, bf16[4,16,1024]{2,1,0:T(8,128)(2,1)}) custom-call(bf16[8,16,1024]{2,1,0:T(8,128)(2,1)} %copy-done.1, bf16[112,1024]{1,0:T(8,128)(2,1)} %copy-done.8), custom_call_target="tpu_custom_call" | custom-call | tf_op jit(solution)/shard_map/halo/pallas_call | solution.py:191
  174.0 1.0 slice_bitcast_fusion.4
  175.0 0.9 fusion.154
  177.2 4.8 %fusion.140 = bf16[1,1,8,16,1024]{4,3,2,1,0:T(8,128)(2,1)} fusion(bf16[11,22,1024]{2,1,0:T(8,128)(2,1)S(1)} %get-tuple-element.99, f32[1024]{0:T(1024)S(1)} %bitcast.348, f32[1024]{0:T(1024)S(1)} %bitcast.350, f32[1024]{0:T(1024)S(1)} %bitcast.352, f32[1024]{0:T(1024)S(1)} %bitcast.354, f32[1024]{0:T(1024)S(1)} %bitcast.356, f32[1024]{0:T(1024)S(1)} %bitcast.358, ...), kind=kLoop, calls=%fused_computation.273 | loop fusion | flops 21889024 | bytes 12095488 | tf_op jit(solution)/shard_map/reshape | solution.py:613
  (313 shorter events, 4.6 us)
Async XLA Ops:
  39.2 6.9 %copy-start.13 = (f32[1,1024]{1,0:T(1,128)}, f32[1,1024]{1,0:T(1,128)S(1)}, u32[]{:S(2)}) copy-start(f32[1,1024]{1,0:T(1,128)S(1)} %get-tuple-element.147) | copy-start | bytes 12292
  39.2 6.9 %copy-start.15 = (f32[1,1024]{1,0:T(1,128)}, f32[1,1024]{1,0:T(1,128)S(1)}, u32[]{:S(2)}) copy-start(f32[1,1024]{1,0:T(1,128)S(1)} %get-tuple-element.148) | copy-start | bytes 12292
  39.2 6.9 %copy-start.17 = (f32[1,1024]{1,0:T(1,128)}, f32[1,1024]{1,0:T(1,128)S(1)}, u32[]{:S(2)}) copy-start(f32[1,1024]{1,0:T(1,128)S(1)} %get-tuple-element.149) | copy-start | bytes 12292
  39.2 6.9 %copy-start.19 = (f32[1,1024]{1,0:T(1,128)}, f32[1,1024]{1,0:T(1,128)S(1)}, u32[]{:S(2)}) copy-start(f32[1,1024]{1,0:T(1,128)S(1)} %get-tuple-element.150) | copy-start | bytes 12292
  39.2 6.9 %copy-start.21 = (f32[1,1024]{1,0:T(1,128)}, f32[1,1024]{1,0:T(1,128)S(1)}, u32[]{:S(2)}) copy-start(f32[1,1024]{1,0:T(1,128)S(1)} %get-tuple-element.151) | copy-start | bytes 12292
  39.3 6.9 %copy-start.23 = (f32[1,1024]{1,0:T(1,128)}, f32[1,1024]{1,0:T(1,128)S(1)}, u32[]{:S(2)}) copy-start(f32[1,1024]{1,0:T(1,128)S(1)} %get-tuple-element.152) | copy-start | bytes 12292
  39.3 6.9 %copy-start.25 = (f32[1,1024]{1,0:T(1,128)}, f32[1,1024]{1,0:T(1,128)S(1)}, u32[]{:S(2)}) copy-start(f32[1,1024]{1,0:T(1,128)S(1)} %get-tuple-element.153) | copy-start | bytes 12292
  39.9 6.2 %copy-start.27 = (f32[1,1024]{1,0:T(1,128)}, f32[1,1024]{1,0:T(1,128)S(1)}, u32[]{:S(2)}) copy-start(f32[1,1024]{1,0:T(1,128)S(1)} %get-tuple-element.119) | copy-start | bytes 12292
  39.9 6.2 %copy-start.29 = (f32[1,1024]{1,0:T(1,128)}, f32[1,1024]{1,0:T(1,128)S(1)}, u32[]{:S(2)}) copy-start(f32[1,1024]{1,0:T(1,128)S(1)} %get-tuple-element.120) | copy-start | bytes 12292
  39.9 6.3 %copy-start.31 = (f32[1,1024]{1,0:T(1,128)}, f32[1,1024]{1,0:T(1,128)S(1)}, u32[]{:S(2)}) copy-start(f32[1,1024]{1,0:T(1,128)S(1)} %get-tuple-element.121) | copy-start | bytes 12292
  39.9 6.3 %copy-start.33 = (f32[1,1024]{1,0:T(1,128)}, f32[1,1024]{1,0:T(1,128)S(1)}, u32[]{:S(2)}) copy-start(f32[1,1024]{1,0:T(1,128)S(1)} %get-tuple-element.122) | copy-start | bytes 12292
  39.9 6.3 %copy-start.35 = (f32[1,1024]{1,0:T(1,128)}, f32[1,1024]{1,0:T(1,128)S(1)}, u32[]{:S(2)}) copy-start(f32[1,1024]{1,0:T(1,128)S(1)} %get-tuple-element.123) | copy-start | bytes 12292
  39.9 6.3 %copy-start.37 = (f32[1,1024]{1,0:T(1,128)}, f32[1,1024]{1,0:T(1,128)S(1)}, u32[]{:S(2)}) copy-start(f32[1,1024]{1,0:T(1,128)S(1)} %get-tuple-element.124) | copy-start | bytes 12292
  39.9 6.3 %copy-start.39 = (f32[1,1024]{1,0:T(1,128)}, f32[1,1024]{1,0:T(1,128)S(1)}, u32[]{:S(2)}) copy-start(f32[1,1024]{1,0:T(1,128)S(1)} %get-tuple-element.125) | copy-start | bytes 12292
  40.0 6.3 %copy-start.41 = (f32[1,1024]{1,0:T(1,128)}, f32[1,1024]{1,0:T(1,128)S(1)}, u32[]{:S(2)}) copy-start(f32[1,1024]{1,0:T(1,128)S(1)} %get-tuple-element.126) | copy-start | bytes 12292
  40.0 6.3 %copy-start.43 = (f32[1,1024]{1,0:T(1,128)}, f32[1,1024]{1,0:T(1,128)S(1)}, u32[]{:S(2)}) copy-start(f32[1,1024]{1,0:T(1,128)S(1)} %get-tuple-element.127) | copy-start | bytes 12292
  40.0 6.3 %copy-start.45 = (f32[1,1024]{1,0:T(1,128)}, f32[1,1024]{1,0:T(1,128)S(1)}, u32[]{:S(2)}) copy-start(f32[1,1024]{1,0:T(1,128)S(1)} %get-tuple-element.128) | copy-start | bytes 12292
  40.0 6.3 %copy-start.47 = (f32[1,1024]{1,0:T(1,128)}, f32[1,1024]{1,0:T(1,128)S(1)}, u32[]{:S(2)}) copy-start(f32[1,1024]{1,0:T(1,128)S(1)} %get-tuple-element.129) | copy-start | bytes 12292
  40.0 6.3 %copy-start.49 = (f32[1,1024]{1,0:T(1,128)}, f32[1,1024]{1,0:T(1,128)S(1)}, u32[]{:S(2)}) copy-start(f32[1,1024]{1,0:T(1,128)S(1)} %get-tuple-element.130) | copy-start | bytes 12292
  40.0 6.3 %copy-start.51 = (f32[1,1024]{1,0:T(1,128)}, f32[1,1024]{1,0:T(1,128)S(1)}, u32[]{:S(2)}) copy-start(f32[1,1024]{1,0:T(1,128)S(1)} %get-tuple-element.131) | copy-start | bytes 12292
  40.0 6.3 %copy-start.53 = (f32[1,1024]{1,0:T(1,128)}, f32[1,1024]{1,0:T(1,128)S(1)}, u32[]{:S(2)}) copy-start(f32[1,1024]{1,0:T(1,128)S(1)} %get-tuple-element.132) | copy-start | bytes 12292
  40.0 6.3 %copy-start.55 = (f32[1,1024]{1,0:T(1,128)}, f32[1,1024]{1,0:T(1,128)S(1)}, u32[]{:S(2)}) copy-start(f32[1,1024]{1,0:T(1,128)S(1)} %get-tuple-element.133) | copy-start | bytes 12292
  40.0 6.3 %copy-start.57 = (f32[1,1024]{1,0:T(1,128)}, f32[1,1024]{1,0:T(1,128)S(1)}, u32[]{:S(2)}) copy-start(f32[1,1024]{1,0:T(1,128)S(1)} %get-tuple-element.134) | copy-start | bytes 12292
  40.1 6.2 %copy-start.59 = (f32[1,1024]{1,0:T(1,128)}, f32[1,1024]{1,0:T(1,128)S(1)}, u32[]{:S(2)}) copy-start(f32[1,1024]{1,0:T(1,128)S(1)} %get-tuple-element.155) | copy-start | bytes 12292
  40.1 6.2 %copy-start.61 = (f32[1,1024]{1,0:T(1,128)}, f32[1,1024]{1,0:T(1,128)S(1)}, u32[]{:S(2)}) copy-start(f32[1,1024]{1,0:T(1,128)S(1)} %get-tuple-element.156) | copy-start | bytes 12292
  40.1 6.2 %copy-start.63 = (f32[1,1024]{1,0:T(1,128)}, f32[1,1024]{1,0:T(1,128)S(1)}, u32[]{:S(2)}) copy-start(f32[1,1024]{1,0:T(1,128)S(1)} %get-tuple-element.157) | copy-start | bytes 12292
  40.1 6.2 %copy-start.65 = (f32[1,1024]{1,0:T(1,128)}, f32[1,1024]{1,0:T(1,128)S(1)}, u32[]{:S(2)}) copy-start(f32[1,1024]{1,0:T(1,128)S(1)} %get-tuple-element.158) | copy-start | bytes 12292
  40.1 6.2 %copy-start.67 = (f32[1,1024]{1,0:T(1,128)}, f32[1,1024]{1,0:T(1,128)S(1)}, u32[]{:S(2)}) copy-start(f32[1,1024]{1,0:T(1,128)S(1)} %get-tuple-element.159) | copy-start | bytes 12292
  40.2 6.2 %copy-start.69 = (f32[1,1024]{1,0:T(1,128)}, f32[1,1024]{1,0:T(1,128)S(1)}, u32[]{:S(2)}) copy-start(f32[1,1024]{1,0:T(1,128)S(1)} %get-tuple-element.160) | copy-start | bytes 12292
  40.2 6.2 %copy-start.71 = (f32[1,1024]{1,0:T(1,128)}, f32[1,1024]{1,0:T(1,128)S(1)}, u32[]{:S(2)}) copy-start(f32[1,1024]{1,0:T(1,128)S(1)} %get-tuple-element.161) | copy-start | bytes 12292
  40.2 6.2 %copy-start.73 = (f32[1,1024]{1,0:T(1,128)}, f32[1,1024]{1,0:T(1,128)S(1)}, u32[]{:S(2)}) copy-start(f32[1,1024]{1,0:T(1,128)S(1)} %get-tuple-element.162) | copy-start | bytes 12292
  40.2 6.2 %copy-start.75 = (f32[1,1024]{1,0:T(1,128)}, f32[1,1024]{1,0:T(1,128)S(1)}, u32[]{:S(2)}) copy-start(f32[1,1024]{1,0:T(1,128)S(1)} %get-tuple-element.163) | copy-start | bytes 12292
  (90 other events, 135.6 us)

commit v2 on v0

v2 whole, which is shorter than its diff:
```python
import functools

import jax
import jax.numpy as jnp
from jax import lax
from jax.experimental import pallas as pl
from jax.experimental.pallas import tpu as pltpu
from jax.sharding import PartitionSpec as P

KS = 7
GX = 4
NX, NY, NZ = 4, 8, 8
MESH = pl.DeviceIdType.MESH
VMEM = pl.BlockSpec(memory_space=pltpu.VMEM)
F32 = jnp.float32
BF16 = jnp.bfloat16
DMA = pltpu.SemaphoreType.DMA


def place():
    dp = lax.axis_index("dp")
    tile = lax.axis_index("tile")
    x = lax.rem(dp, 4)
    y = lax.div(tile, 16) * 4 + lax.div(dp, 4)
    z = lax.rem(lax.div(tile, 2), 8)
    core = lax.rem(tile, 2)
    return x, y, z, core


def device(x, y, z, core):
    return (lax.rem(y, 4) * 4 + x, lax.div(y, 4) * 16 + z * 2 + core)


def turned(index, by, size):
    return lax.rem(index + (by % size), size)


def greet(barrier, peer):
    pl.semaphore_signal(barrier, inc=1, device_id=peer, device_id_type=MESH)


def remote(src, dst, ssem, rsem, peer):
    return pltpu.make_async_remote_copy(
        src_ref=src, dst_ref=dst, send_sem=ssem, recv_sem=rsem, device_id=peer, device_id_type=MESH
    )


STEPS = [(-1, 0), (1, 0), (0, -1), (0, 1), (-1, -1), (-1, 1), (1, -1), (1, 1)]


def halo_sides():
    dp = lax.axis_index("dp")
    tile = lax.axis_index("tile")
    ty = lax.div(tile, GX)
    tx = lax.rem(tile, GX)
    sides = []
    for dr, dc in STEPS:
        there = None
        for ok in ([ty >= 1] if dr < 0 else [ty <= 6] if dr > 0 else []) + (
            [tx >= 1] if dc < 0 else [tx <= 2] if dc > 0 else []
        ):
            there = ok if there is None else there & ok
        sides.append((there, (dp, tile + dr * GX + dc)))
    return sides


OFF4 = [0, -1, 1, 2]
OFF8 = [0, -1, 1, -2, 2, -3, 3, 4]


def ring_slots(n, count):
    half = n // 2
    right = [(s, j) for s in range(1, half) for j in range(count)] + [(half, j) for j in range(count // 2)]
    left = [(s, j) for s in range(1, half) for j in range(count)] + [(half, j) for j in range(count // 2, count)]
    return right, left


class Ring:
    def __init__(self, n, count, offs, sub, peers, ssem, rsem, wire):
        self.n, self.count, self.offs, self.sub, self.peers = n, count, offs, sub, peers
        self.ssem, self.rsem, self.wire = ssem, rsem, wire
        self.slots = ring_slots(n, count)

    def copy(self, way, s, j):
        i = self.slots[way].index((s, j))
        ref = self.sub(-(s - 1) if way == 0 else (s - 1), j)
        return remote(ref, ref, self.ssem.at[way, i], self.rsem.at[way, i], self.peers[way])

    def landed(self, way, s, j):
        i = self.slots[way].index((s, j))
        ref = self.sub(-s if way == 0 else s, j)
        return pltpu.make_async_copy(ref, ref, self.rsem.at[way, i])


def plan(outer, inner):
    events = []
    latency = 1.7
    for c, (o, i) in enumerate(zip(outer, inner)):
        ready = {0: 0.0}
        for way in (0, 1):
            t, got = 0.0, {}
            for s, j in i.slots[way]:
                t = max(t, 0.0 if s == 1 else got[s - 1, j]) + i.wire
                got[s, j] = t + latency
                events.append((got[s, j], c, 0, way, s, j))
        for way in (0, 1):
            for s, j in i.slots[way]:
                pass
        half = i.n // 2
        seen = {(e[3], e[4], e[5]): e[0] for e in events if e[1] == c and e[2] == 0}
        for k, off in enumerate(o.offs):
            if off == 0:
                continue
            if abs(off) == half:
                ready[k] = max(v for (w, s, j), v in seen.items() if s == half)
            else:
                ready[k] = max(v for (w, s, j), v in seen.items() if s == abs(off) and w == (0 if off < 0 else 1))
        for way in (0, 1):
            t, got = 0.0, {}
            for s, j in o.slots[way]:
                t = max(t, ready[j] if s == 1 else got[s - 1, j]) + o.wire
                got[s, j] = t + latency
                events.append((got[s, j], c, 1, way, s, j))
    return sorted(events)


def halo_count():
    count = 0
    for there, _ in halo_sides():
        count = count + there.astype(jnp.int32)
    return count


BACK = [1, 0, 3, 2, 7, 6, 5, 4]


class Halo:
    def __init__(self, grid, ecol, ecor, rows, cols, cors, ssem, rsem):
        self.grid, self.ecol, self.ecor = grid, ecol, ecor
        self.rows, self.cols, self.cors = rows, cols, cors
        src = [grid.at[:, 0:3], grid.at[:, 5:8], ecol.at[0], ecol.at[1]] + [ecor.at[k] for k in range(4)]
        self.dst = [rows.at[1], rows.at[0], cols.at[1], cols.at[0], cors.at[3], cors.at[2], cors.at[1], cors.at[0]]
        self.rsem = rsem
        self.moves = []
        for k, (there, peer) in enumerate(halo_sides()):
            self.moves.append((there, remote(src[k], self.dst[k], ssem.at[k], rsem.at[BACK[k]], peer)))

    def start(self):
        for there, copy in self.moves:
            @pl.when(there)
            def _():
                copy.start()

    def finish(self):
        for k, (there, copy) in enumerate(self.moves):
            landed = self.dst[BACK[k]]
            @pl.when(there)
            def _():
                pltpu.make_async_copy(landed, landed, self.rsem.at[k]).wait()
                copy.wait_send()

            @pl.when(jnp.logical_not(there))
            def _():
                landed[...] = jnp.zeros(landed.shape, landed.dtype)

    def cut(self, cb, value, stage):
        for i in range(8):
            stage[3 * i : 3 * i + 3, :] = value[i, 0:3, :]
            stage[24 + 3 * i : 27 + 3 * i, :] = value[i, 13:16, :]
        for k, (r, c) in enumerate(((0, 0), (0, 13), (5, 0), (5, 13))):
            for i in range(3):
                at = 48 + 16 * k + 3 * i
                stage[at : at + 3, :] = value[r + i, c : c + 3, :]
        self.ecol[0, cb] = stage[0:24, :].astype(BF16)
        self.ecol[1, cb] = stage[24:48, :].astype(BF16)
        for k in range(4):
            self.ecor[k, cb] = stage[48 + 16 * k : 64 + 16 * k, :].astype(BF16)

    def fill(self, cb, pad):
        pad[cb, 3:11, 8:24, :] = self.grid[cb].astype(F32)
        pad[cb, 0:3, 8:24, :] = self.rows[0, cb].astype(F32)
        pad[cb, 11:14, 8:24, :] = self.rows[1, cb].astype(F32)
        for side, col in ((0, 5), (1, 24)):
            value = self.cols[side, cb].astype(F32)
            for i in range(8):
                pad[cb, 3 + i, col : col + 3, :] = value[3 * i : 3 * i + 3, :]
        for k, (row, col) in enumerate(((0, 5), (0, 24), (11, 5), (11, 24))):
            value = self.cors[k, cb].astype(F32)
            for i in range(3):
                pad[cb, row + i, col : col + 3, :] = value[3 * i : 3 * i + 3, :]


def each(count, body):
    def step(i, carry):
        body(i)
        return carry

    lax.fori_loop(0, count, step, 0)


def block_conv(start, pad, taps, cb, flip):
    total = start
    for b in range(KS):
        window = pad[cb, :, 5 + b : 21 + b, :]
        for a in range(KS):
            tap = (6 - a) * KS + (6 - b) if flip else a * KS + b
            total = total + taps[cb, tap : tap + 1, :][None] * window[a : a + 8]
    return total


LAST = 5
CHUNKS = [
    [(0, 0), (2, 0), (1, 0)],
    [(0, -1), (0, 1), (2, -1), (2, 1)],
    [(1, -1), (1, 1)],
    [(0, -2), (0, 2), (2, -2), (2, 2)],
    [(0, -3), (0, 3), (2, -3), (2, 3)],
    [(0, 4), (2, 4), (1, 2)],
]


def whole_body(
    field, cot, wt, par, bia,
    block_out, grad_in, out_kernel, out_vec,
    fb, cb_, ecol, ecor, stage, hrows, hcols, hcors, wrows, wcols, wcors, pad, bpad, pars, taps, row, zbias, bias, table,
    rz, ry, scr, g0, g1, g2, act, hid, acc, part, mypart, conv, inv, bc, wire, ob, sums,
    r1, r2, r3, mid, low, fin, tot,
    ls, hs, hr, h2s, h2r, ps, pr, zs, zr, bs, br, as_, ar, s0s, s0r, p1s, p1r,
    q0s, q0r, q1s, q1r, q2s, q2r, r0s, r0r, r1s, r1r, r2s, r2r, es, er,
    s1, t1, s2, t2, s3, t3, s4, t4, os_,
):
    x, y, z, core = place()
    dp = lax.axis_index("dp")
    tile = lax.axis_index("tile")
    yl, yh = lax.rem(y, 4), lax.div(y, 4)
    xl, xh = lax.rem(x, 2), lax.div(x, 2)
    lane = lax.broadcasted_iota(jnp.int32, (1, 128), 1)
    barrier = pltpu.get_barrier_semaphore()
    sibling = device(x, y, z, 1 - core)
    xps = [device(turned(x, k, NX), y, z, core) for k in range(1, NX)]
    yps = [device(x, turned(y, k, NY), z, core) for k in range(1, NY)]
    zps = [device(x, y, turned(z, k, NZ), core) for k in range(1, NZ)]
    dps = [(turned(dp, k, 16), tile) for k in range(1, 16)]
    xys = [device(turned(x, k % 4, NX), turned(y, k // 4, NY), z, core) for k in range(1, 32)]
    mine = yl * 2 + xh
    member = yh * 4 + xl * 2 + core
    thirds = []
    for k in range(1, 8):
        o = turned(member, k, 8)
        thirds.append(device(xh * 2 + lax.rem(lax.div(o, 2), 2), lax.div(o, 4) * 4 + yl, z, lax.rem(o, 2)))
    for peer in xys + zps + thirds[0::2]:
        greet(barrier, peer)
    for there, peer in halo_sides():
        @pl.when(there)
        def _():
            greet(barrier, peer)

    loads = []
    for cb in range(8):
        lanes = pl.ds(128 * cb, 128)
        loads.append(pltpu.make_async_copy(field.at[:, :, lanes], fb.at[cb], ls.at[0, cb]))
        loads.append(pltpu.make_async_copy(cot.at[:, lanes], cb_.at[cb], ls.at[1, cb]))
    for copy in loads:
        copy.start()
    halo1 = Halo(fb, ecol, ecor, hrows, hcols, hcors, hs, hr)
    for copy in loads:
        copy.wait()
    pl.semaphore_wait(barrier, 31 + 7 + 4 + halo_count())

    zero = []
    for k in range(1, NZ):
        zero.append(remote(wt.at[turned(z, k, NZ)], rz.at[z], s0s.at[0, k - 1], s0r.at[0, k - 1], zps[k - 1]))
    for k in range(1, NY):
        zero.append(remote(wt.at[turned(y, k, NY)], ry.at[y], s0s.at[1, k - 1], s0r.at[1, k - 1], yps[k - 1]))
    for copy in zero:
        copy.start()
    zcp = [remote(bia, zbias.at[z], zs.at[k], zr.at[k], peer) for k, peer in enumerate(zps)]
    for copy in zcp:
        copy.start()
    pcp = [remote(par, pars.at[dp], ps.at[k], pr.at[k], peer) for k, peer in enumerate(dps)]
    for copy in pcp:
        copy.start()
    rz[z] = wt[z]
    ry[y] = wt[y]
    zbias[z] = bia[...]
    pars[dp] = par[...]
    stage[...] = jnp.zeros_like(stage)
    each(8, lambda cb: halo1.cut(cb, fb[cb].astype(F32), stage))
    halo1.start()

    for copy in zero:
        copy.wait()
    home = (g0.at[y, x, z], g1.at[x, z, y], g2.at[z, y, x])
    for k in range(3):
        src = (rz, ry, ry)[k]
        for d in range(8):
            val = src[d].astype(F32)
            scr[k, 0, 2 * d : 2 * d + 2, :] = val[2 * k : 2 * k + 2]
            scr[k, 1, 2 * d : 2 * d + 2, :] = val[6 + 2 * k : 8 + 2 * k]
        home[k][...] = scr[k].astype(BF16)
    first = []
    for k, peers in enumerate((zps, yps, xps)):
        line = [remote(home[k], home[k], p1s.at[k, i], p1r.at[k, i], peer) for i, peer in enumerate(peers)]
        for copy in line:
            copy.start()
        first.append(line)

    for copy in zcp:
        copy.wait()
    total = zbias[0]
    for k in range(1, NZ):
        total = total + pltpu.roll(zbias[k], 6 * k, 1)
    row[...] = total
    me = x * 8 + y
    bias[me] = total
    bcp = [remote(row, bias.at[me], bs.at[k], br.at[k], peer) for k, peer in enumerate(xys)]
    for copy in bcp:
        copy.start()

    xr, xb = xps[0], xps[-1]
    yr, yb = yps[0], yps[-1]
    zr_, zb = zps[0], zps[-1]
    inner = [
        Ring(4, 2, OFF4, lambda b, j: g0.at[y, turned(x, b, 4), pl.ds(4 * j, 4)], (xr, xb), q0s, q0r, 0.7),
        Ring(8, 2, OFF8, lambda b, j: g1.at[x, turned(z, b, 8), pl.ds(4 * j, 4)], (zr_, zb), q1s, q1r, 0.7),
        Ring(8, 2, OFF8, lambda b, j: g2.at[z, turned(y, b, 8), pl.ds(2 * j, 2)], (yr, yb), q2s, q2r, 0.35),
    ]
    outer = [
        Ring(8, 4, OFF4, lambda b, j: g0.at[turned(y, b, 8), turned(x, OFF4[j], 4)], (yr, yb), r0s, r0r, 1.4),
        Ring(4, 8, OFF8, lambda b, j: g1.at[turned(x, b, 4), turned(z, OFF8[j], 8)], (xr, xb), r1s, r1r, 1.4),
        Ring(8, 8, OFF8, lambda b, j: g2.at[turned(z, b, 8), turned(y, OFF8[j], 8)], (zr_, zb), r2s, r2r, 0.7),
    ]
    started = []

    def go(copy):
        copy.start()
        started.append(copy)

    def arrive(k, level, way, s, j):
        ring = (inner, outer)[level][k]
        ring.landed(way, s, j).wait()
        if (s + 1, j) in ring.slots[way]:
            go(ring.copy(way, s + 1, j))
        half = ring.n // 2
        if level == 0 and j == (1 if s < half else way) and not (s == half and way == 0):
            index = ring.offs.index(half if s == half else -s if way == 0 else s)
            for w in (0, 1):
                if (1, index) in outer[k].slots[w]:
                    go(outer[k].copy(w, 1, index))

    ship = [remote(act.at[a, core], act.at[a, core], as_.at[a], ar.at[a], sibling) for a in range(2)]

    def params():
        for copy in pcp:
            copy.wait()

        def unpack(cb):
            one, two = pars[2 * cb], pars[2 * cb + 1]
            taps[cb, 0:28, :] = jnp.where(lane < 64, one, pltpu.roll(two, 64, 1))
            taps[cb, 28:56, :] = jnp.where(lane < 64, pltpu.roll(one, 64, 1), two)

        each(8, unpack)
        for cb in range(8):
            scaled = cb_[cb].astype(F32) * taps[cb, 52:53, :]
            act[1, core, :, 128 * cb : 128 * cb + 128] = scaled.astype(BF16)

    def borders():
        ship[1].start()
        halo1.finish()
        each(8, lambda cb: halo1.fill(cb, pad))

    def conv_piece(part_number):
        def one(i):
            cb = i + 2 * part_number
            start = jnp.broadcast_to(taps[cb, 49:50, :][None], (8, 16, 128))
            conv[cb] = block_conv(start, pad, taps, cb, False).reshape(128, 128)

        each(2, one)

    def norm():
        mean = jnp.sum(sum(conv[cb] for cb in range(8)), axis=-1, keepdims=True) * (1.0 / 1024)
        square = jnp.zeros((128, 128), F32)
        for cb in range(8):
            centered = conv[cb] - mean
            square = square + centered * centered
        inverse = lax.rsqrt(jnp.sum(square, axis=-1, keepdims=True) * (1.0 / 1024) + 1e-06)
        inv[...] = jnp.broadcast_to(inverse, (128, 128))
        for cb in range(8):
            standard = (conv[cb] - mean) * inverse
            conv[cb] = standard
            normed = standard * taps[cb, 50:51, :] + taps[cb, 51:52, :]
            act[0, core, :, 128 * cb : 128 * cb + 128] = normed.astype(BF16)

    def biases():
        ship[0].start()
        for copy in bcp:
            copy.wait()
        values = bias[...].reshape(32, 128).astype(BF16)
        j = lax.broadcasted_iota(jnp.int32, (128, 128), 0)
        l = lax.broadcasted_iota(jnp.int32, (128, 128), 1)
        bx = lax.broadcasted_iota(jnp.int32, (4, 8, 128), 0)
        by = lax.broadcasted_iota(jnp.int32, (4, 8, 128), 1)
        bl = lax.broadcasted_iota(jnp.int32, (4, 8, 128), 2)
        l64 = bl & 63

        def pick(where):
            chosen = jnp.where(where, 1.0, 0.0).astype(BF16)
            return jnp.dot(values, chosen, preferred_element_type=F32).reshape(4, 8, 128)

        t0 = pick(j == 6 * ((l >> 1) & 7) + (l & 1))
        table[0] = jnp.sum(jnp.where(bx == (l64 >> 4), t0, 0.0), axis=0)
        t1_ = pick(j == 6 * (l >> 4) + 2 + (l & 1))
        table[1, 0:4, :] = jnp.sum(jnp.where(by == ((bl >> 1) & 7), t1_, 0.0), axis=1)
        for zz in range(8):
            t2_ = pick(j == 6 * zz + 4 + (l & 1))
            kept = jnp.where((bx == (l64 >> 4)) & (by == ((bl >> 1) & 7)), t2_, 0.0)
            table[2, zz : zz + 1, :] = jnp.sum(jnp.sum(kept, axis=0), axis=0, keepdims=True)
        for copy in ship:
            copy.wait()

    at = (lambda off: turned(y, off, 8), lambda off: turned(x, off, 4), lambda off: turned(z, off, 8))
    nt = (((1,), (1,)), ((), ()))

    def weights(blocks, m):
        columns = []
        for cb in range(8):
            pieces = []
            for k, off in blocks:
                if k == 0:
                    pieces.append(g0[at[0](off), :, cb, m].reshape(64, 128))
                elif k == 1:
                    pieces.append(g1[at[1](off), :, cb, m].reshape(128, 128))
                else:
                    pieces.append(g2[at[2](off), cb, :, m].reshape(64, 128))
            columns.append(jnp.concatenate(pieces, axis=0))
        return jnp.concatenate(columns, axis=1)

    def bias_row(blocks):
        out, pend = [], None
        for k, off in blocks:
            value = table[k, pl.ds(at[k](off), 1), :]
            if k == 1:
                out.append(value)
            elif pend is None:
                pend = value
            else:
                out.append(jnp.where(lane < 64, pend, value))
                pend = None
        return jnp.concatenate(out, axis=1)

    def front(blocks, a_in, a_out):
        pre = lax.dot_general(a_in, weights(blocks, 0), nt, preferred_element_type=F32) + bias_row(blocks)
        back = lax.dot_general(a_out, weights(blocks, 1), nt, preferred_element_type=F32)
        cdf = 0.5 * (1.0 + lax.erf(pre * 0.7071067811865476))
        slope = cdf + pre * jnp.exp(-0.5 * pre * pre) * 0.3989422804014327
        return (pre * cdf).astype(BF16), (back * slope).astype(BF16)

    def chunk_front(n):
        hidden, back_pre = front(CHUNKS[n], act[0].reshape(256, 1024), act[1].reshape(256, 1024))
        hid[0], hid[1] = hidden, back_pre

    def chunk_back(n):
        for m in range(2):
            value = jnp.dot(hid[m], weights(CHUNKS[n], 1 - m), preferred_element_type=F32).reshape(2, 128, 1024)
            for cb in range(8):
                piece = value[:, :, 128 * cb : 128 * cb + 128]
                acc[m, :, cb] = piece if n == 0 else acc[m, :, cb] + piece

    tasks = [(0.7, None, functools.partial(conv_piece, i)) for i in range(4)]
    tasks += [(1.0, None, norm), (0.8, None, biases)]
    for n in range(LAST):
        tasks.append((1.2, CHUNKS[n], functools.partial(chunk_front, n)))
        tasks.append((1.0, CHUNKS[n], functools.partial(chunk_back, n)))
    params()
    borders()
    for k in range(3):
        for copy in first[k]:
            copy.wait()
        for way in (0, 1):
            go(outer[k].copy(way, 1, 0))
            for j in range(2):
                go(inner[k].copy(way, 1, j))
    events = plan(outer, inner)

    def needs(event, blocks):
        _, k, level, way, s, j = event
        if blocks is None:
            return False
        for kk, off in blocks:
            if kk != k:
                continue
            if off == 0 and level == 0:
                return True
            if off != 0 and level == 1 and (abs(off) == s) and (s == outer[k].n // 2 or (off < 0) == (way == 0)):
                return True
        return False

    clock = 0.0
    while events or tasks:
        ready = bool(tasks) and not any(needs(e, tasks[0][1]) for e in events)
        if events and (events[0][0] <= clock or not ready):
            event = events.pop(0)
            clock = max(clock, event[0])
            arrive(*event[1:])
        else:
            length, _, piece = tasks.pop(0)
            piece()
            clock += length

    blocks = CHUNKS[LAST]
    swap = [remote(mypart.at[a], part.at[a], es.at[a], er.at[a], sibling) for a in range(2)]
    for turn, who in enumerate((1 - core, core)):
        for m, h in enumerate(front(blocks, act[0, who], act[1, who])):
            hid[m, 0:128, :] = h
        for m in range(2):
            value = jnp.dot(hid[m, 0:128, :], weights(blocks, 1 - m), preferred_element_type=F32)
            for cb in range(8):
                piece = acc[m, who, cb] + value[:, 128 * cb : 128 * cb + 128]
                if turn == 0:
                    mypart[m, cb] = piece.astype(BF16)
                else:
                    acc[m, core, cb] = piece
            if turn == 0:
                swap[m].start()
    for copy in swap:
        copy.wait_recv()

    sums[:, 48:64, :] = jnp.zeros((8, 16, 128), F32)

    def down(value):
        return jnp.sum(value, axis=0, keepdims=True)

    def ending(cb, carry):
        one, two = carry
        standard = conv[cb]
        upstream = cb_[cb].astype(F32)
        projected = acc[0, core, cb] + part[0, cb].astype(F32) + taps[cb, 53:54, :]
        normed = acc[1, core, cb] + part[1, cb].astype(F32)
        source = fb[cb].astype(F32).reshape(128, 128)
        ob[0, cb] = (source + taps[cb, 52:53, :] * projected).astype(BF16)
        sums[cb, 50:51, :] = down(normed * standard)
        sums[cb, 51:52, :] = down(normed)
        sums[cb, 52:53, :] = down(upstream * projected)
        scaled = normed * taps[cb, 50:51, :]
        bc[cb] = scaled
        return one + scaled, two + scaled * standard

    none = jnp.zeros((128, 128), F32)
    one, two = lax.fori_loop(0, 8, ending, (none, none))
    mean_one = jnp.sum(one, axis=-1, keepdims=True) * (1.0 / 1024)
    mean_two = jnp.sum(two, axis=-1, keepdims=True) * (1.0 / 1024)
    halo2 = Halo(wire, ecol, ecor, wrows, wcols, wcors, h2s, h2r)
    inverse = inv[...]

    def rear(cb):
        back = inverse * (bc[cb] - mean_one - conv[cb] * mean_two)
        bc[cb] = back
        sums[cb, 49:50, :] = down(back)
        back = back.reshape(8, 16, 128)
        wire[cb] = back.astype(BF16)
        halo2.cut(cb, back, stage)

    each(8, rear)
    halo2.start()
    puts = []
    for cb in range(8):
        puts.append(pltpu.make_async_copy(ob.at[0, cb], block_out.at[:, pl.ds(128 * cb, 128)], os_.at[0, cb]))
        puts[-1].start()

    def block_grad(cb):
        back = bc[cb].reshape(8, 16, 128)
        for b in range(KS):
            window = pad[cb, :, 5 + b : 21 + b, :]
            for a in range(KS):
                product = jnp.sum(back * window[a : a + 8], axis=0)
                sums[cb, a * KS + b : a * KS + b + 1, :] = down(product)

    def firsts(k):
        other = lax.rem(mine + k, 8)
        peer = device(lax.rem(other, 2) * 2 + xl, yh * 4 + lax.div(other, 2), z, core)
        return other, remote(sums.at[other], r1.at[mine], s1.at[k - 1], t1.at[k - 1], peer)

    def grad_step(i):
        other, copy = firsts(i + 1)
        block_grad(other)
        copy.start()

    each(7, grad_step)
    block_grad(mine)
    r1[mine] = sums[mine]
    halo2.finish()

    def conv_back(low_, count):
        def one(i):
            cb = i + low_
            halo2.fill(cb, bpad)
            start = cb_[cb].astype(F32).reshape(8, 16, 128)
            ob[1, cb] = block_conv(start, bpad, taps, cb, True).reshape(128, 128).astype(BF16)

        each(count, one)
        for cb in range(low_, low_ + count):
            puts.append(pltpu.make_async_copy(ob.at[1, cb], grad_in.at[:, pl.ds(128 * cb, 128)], os_.at[1, cb]))
            puts[-1].start()

    conv_back(0, 2)
    for k in range(1, 8):
        firsts(k)[1].wait()
    mid[...] = jnp.sum(r1[...], axis=0).reshape(8, 8, 128)
    c2 = [remote(mid.at[turned(z, k + 1, 8)], r2.at[z], s2.at[k], t2.at[k], zps[k]) for k in range(7)]
    for copy in c2:
        copy.start()
    r2[z] = mid[z]
    conv_back(2, 3)
    for copy in c2:
        copy.wait()
    low[...] = jnp.sum(r2[...], axis=0)
    c3 = [remote(low, r3.at[member], s3.at[k], t3.at[k], thirds[k]) for k in range(7)]
    for copy in c3:
        copy.start()
    r3[member] = low[...]
    conv_back(5, 3)
    for copy in c3:
        copy.wait()
    fin[...] = jnp.sum(r3[...], axis=0)
    c4 = [remote(fin, tot.at[z], s4.at[k], t4.at[k], zps[k]) for k in range(7)]
    for copy in c4:
        copy.start()
    tot[z] = fin[...]
    for copy in started + swap:
        copy.wait_send()
    for copy in puts:
        copy.wait()
    for copy in c4:
        copy.wait()
    final = tot[...].reshape(64, 128) * (1.0 / 256.0)
    final = jnp.where(xl == 0, final, pltpu.roll(final, 64, 1))
    out_kernel[...] = final[0:49, 0:64]
    out_vec[...] = final[48:56, 0:64]


def whole(field, cot, wt, par, bia):
    cell = (2, 16, 128)
    any_ = pl.BlockSpec(memory_space=pl.ANY)
    scratch = [
        ((8, 8, 16, 128), BF16), ((8, 128, 128), BF16), ((2, 8, 24, 128), BF16), ((4, 8, 16, 128), BF16), ((112, 128), F32),
        ((2, 8, 3, 16, 128), BF16), ((2, 8, 24, 128), BF16), ((4, 8, 16, 128), BF16),
        ((2, 8, 3, 16, 128), BF16), ((2, 8, 24, 128), BF16), ((4, 8, 16, 128), BF16),
        ((8, 14, 32, 128), F32), ((8, 14, 32, 128), F32), ((16, 28, 128), F32), ((8, 56, 128), F32),
        ((1, 128), F32), ((8, 1, 128), F32), ((32, 1, 128), F32), ((3, 8, 128), F32),
        ((8, 16, 128), BF16), ((8, 16, 128), BF16), ((3, 2, 16, 128), F32),
        ((8, 4, 8) + cell, BF16), ((4, 8, 8) + cell, BF16), ((8, 8, 4) + cell, BF16),
        ((2, 2, 128, 1024), BF16), ((2, 256, 256), BF16), ((2, 2, 8, 128, 128), F32),
        ((2, 8, 128, 128), BF16), ((2, 8, 128, 128), BF16), ((8, 128, 128), F32), ((128, 128), F32),
        ((8, 128, 128), F32), ((8, 8, 16, 128), BF16), ((2, 8, 128, 128), BF16), ((8, 64, 128), F32),
        ((8, 64, 128), F32), ((8, 8, 128), F32), ((8, 8, 128), F32), ((8, 8, 128), F32), ((8, 128), F32), ((8, 128), F32),
        ((8, 8, 128), F32),
    ]
    sems = [(2, 8), (8,), (8,), (8,), (8,), (15,), (15,), (7,), (7,), (31,), (31,), (2,), (2,), (2, 7), (2, 7), (3, 7), (3, 7)]
    sems += [(2, 3), (2, 3), (2, 7), (2, 7), (2, 7), (2, 7), (2, 14), (2, 14), (2, 12), (2, 12), (2, 28), (2, 28), (2,), (2,)]
    sems += [(7,)] * 8 + [(2, 8)]
    return pl.pallas_call(
        whole_body,
        out_shape=(
            jax.ShapeDtypeStruct((128, 1024), BF16),
            jax.ShapeDtypeStruct((128, 1024), BF16),
            jax.ShapeDtypeStruct((49, 64), F32),
            jax.ShapeDtypeStruct((8, 64), F32),
        ),
        in_specs=[any_, any_, VMEM, VMEM, VMEM],
        out_specs=[any_, any_, VMEM, VMEM],
        scratch_shapes=[pltpu.VMEM(*s) for s in scratch] + [DMA(s) for s in sems],
        compiler_params=pltpu.CompilerParams(
            collective_id=0, has_side_effects=True, vmem_limit_bytes=56 * 1024 * 1024
        ),
        name="whole",
    )(field, cot, wt, par, bia)


def per_device(
    features,
    cotangent,
    in_weight,
    out_weight,
    hidden_bias,
    kernel,
    conv_bias,
    norm_gain,
    norm_bias,
    layer_scale,
    out_bias,
):
    _, _, rows, cols, width = features.shape
    field = features.reshape(rows, cols, width)
    cot = cotangent.reshape(rows * cols, width)
    slab = jnp.concatenate(
        [kernel] + [v[None] for v in (conv_bias, norm_gain, norm_bias, layer_scale, out_bias)] + [jnp.zeros((2, 64), F32)]
    )
    par = jnp.concatenate([slab[:28], slab[28:]], axis=1)
    bia = jnp.pad(hidden_bias.astype(F32)[None], ((0, 0), (0, 122)))
    both = jnp.concatenate([in_weight, out_weight, jnp.zeros((4, width), BF16)])
    wt = both.reshape(16, 8, 128).transpose(1, 0, 2)
    block_out, grad_in, out_kernel, out_vec = whole(field, cot, wt, par, bia)
    return (
        block_out.reshape(features.shape),
        grad_in.reshape(features.shape),
        out_kernel,
        out_vec[1],
        out_vec[2],
        out_vec[3],
        out_vec[4],
    )


def solution(mesh):
    placed = (
        P("dp", "tile", None, None, None),
        P("dp", "tile", None, None, None),
        P(("dp", "tile"), None),
        P(("dp", "tile"), None),
        P(("dp", "tile")),
        P(None, "dp"),
        P("dp"),
        P("dp"),
        P("dp"),
        P("dp"),
        P("dp"),
    )
    return jax.shard_map(
        per_device,
        mesh=mesh,
        in_specs=placed,
        out_specs=(
            P("dp", "tile", None, None, None),
            P("dp", "tile", None, None, None),
            P(None, "dp"),
            P("dp"),
            P("dp"),
            P("dp"),
            P("dp"),
        ),
        check_vma=False,
    )
```

time: 2040 us -> 115 us (0.06)
  the two profiles are of different devices: /device:TPU:2 before, /device:TPU:8 now
where the time goes in v2:
time: 115 us
  Pallas kernels  105 us (91%)
  local copies, waits for them, and re-layouts  7.33 us (6%)
  other arithmetic  1.88 us (2%)
    pallas_call x1, Pallas kernels, whole(): pl.pallas_call(whole_body, out_shape=(jax.ShapeDtypeStruct((128, 1024), B...  105 us
    unnamed x23, local copies, waits for them, and re-layouts  4.4 us

profile of v2, /device:TPU:8, one launch (start us, length us, event | category | flops | bytes accessed | tf_op | source)
XLA Modules:
  0.0 114.7 jit_solution(9784779084294337578)
XLA Ops:
  0.6 0.0 copy-start.7
  0.6 0.0 copy-start.8
  0.7 0.0 copy-start.4
  0.7 0.0 copy-start.5
  0.7 0.0 copy-start.6
  0.7 0.6 copy-done.7
  1.3 0.0 copy-done.8
  1.3 0.0 copy-done.4
  1.3 0.0 copy-done.5
  1.3 0.0 copy-done.6
  1.4 0.8 concatenate.10
  2.1 0.0 slice-start
  2.1 0.7 slice-done
  2.9 0.0 copy-start.2
  2.9 0.0 copy-start.3
  2.9 0.7 pad_maximum_fusion.par
  3.5 0.1 pad.12.clone
  3.6 0.0 copy-done.2
  3.6 0.0 copy-done.3
  3.6 0.7 bitcast_bitcast_fusion.wt
  4.3 0.0 copy-start.9
  4.3 0.7 copy-done.9
  5.0 0.5 pad_convert_fusion.bia
  5.5 104.8 %whole.1 = (bf16[128,1024]{1,0:T(8,128)(2,1)}, bf16[128,1024]{1,0:T(8,128)(2,1)}, f32[49,64]{1,0:T(8,128)}, f32[8,64]{1,0:T(8,128)}) custom-call(bf16[8,16,1024]{2,1,0:T(8,128)(2,1)} %bitcast.27, bf16[128,1024]{1,0:T(8,128)(2,1)} %bitcast.28, bf16[8,16,128]{2,1,0:T(8,128)(2,1)} %bitcast_bitcast_fusion.wt, f32[28,128]{1,0:T(8,128)} %pad_maximum_fusion.par, ...), custom_call_target="tpu_custom_call" | custom-call | tf_op jit(solution)/shard_map/whole/pallas_call | solution.py:661
  110.3 1.4 %slice_bitcast_fusion = (f32[64]{0:T(128)}, f32[64]{0:T(128)}, f32[64]{0:T(128)}, f32[64]{0:T(128)}) fusion(f32[8,64]{1,0:T(8,128)} %get-tuple-element.14), kind=kLoop, calls=%fused_computation.3 | loop fusion | bytes 2048 | tf_op jit(solution)/shard_map/squeeze | solution.py:710
  111.6 0.0 copy-start
  111.6 1.7 %copy.24 = bf16[1,1,8,16,1024]{4,3,2,1,0:T(8,128)(2,1)} copy(bf16[1,1,8,16,1024]{4,3,2,1,0:T(8,128)(2,1)} %bitcast.26) | data formatting | bytes 524288
  113.3 0.0 copy-done
  113.3 0.0 copy-start.1
  113.3 0.7 copy.25
  114.0 0.0 copy-done.1
  114.1 0.6 copy.26
  (3 shorter events, 0.0 us)
Async XLA Ops:
  0.6 0.7 copy-start.7
  0.6 0.7 copy-start.8
  0.7 0.7 copy-start.4
  0.7 0.7 copy-start.5
  0.7 0.7 copy-start.6
  2.1 0.7 slice-start
  2.9 0.8 copy-start.2
  2.9 0.8 copy-start.3
  4.3 0.7 copy-start.9
  111.6 1.7 %copy-start = (bf16[128,1024]{1,0:T(8,128)(2,1)S(1)}, bf16[128,1024]{1,0:T(8,128)(2,1)}, u32[]{:S(2)}) copy-start(bf16[128,1024]{1,0:T(8,128)(2,1)} %get-tuple-element.12) | copy-start | bytes 786436
  113.3 0.7 copy-start.1

commit v3 on v2

--- a/solution.py
+++ b/solution.py
@@ -84,7 +84,7 @@
     def copy(self, way, s, j):
         i = self.slots[way].index((s, j))
         ref = self.sub(-(s - 1) if way == 0 else (s - 1), j)
-        return remote(ref, ref, self.ssem.at[way, i], self.rsem.at[way, i], self.peers[way])
+        return remote(ref, ref, self.ssem, self.rsem.at[way, i], self.peers[way])
 
     def landed(self, way, s, j):
         i = self.slots[way].index((s, j))
@@ -220,14 +220,12 @@
 
 
 def whole_body(
-    field, cot, wt, par, bia,
-    block_out, grad_in, out_kernel, out_vec,
-    fb, cb_, ecol, ecor, stage, hrows, hcols, hcors, wrows, wcols, wcors, pad, bpad, pars, taps, row, zbias, bias, table,
-    rz, ry, scr, g0, g1, g2, act, hid, acc, part, mypart, conv, inv, bc, wire, ob, sums,
+    field, cot, w_in, w_out, hbias, taps_in, v0, v1, v2, v3, v4,
+    block_out, grad_in, out_sums,
+    fb, cb_, raw, rawz, rawy, slab, par, bia, ecol, ecor, stage, hrows, hcols, hcors, wrows, wcols, wcors, pad, bpad, pars, taps, row, zbias, bias, table,
+    rz, ry, g0, g1, g2, act, hid, acc, part, mypart, conv, inv, bc, wire, ob, sums,
     r1, r2, r3, mid, low, fin, tot,
-    ls, hs, hr, h2s, h2r, ps, pr, zs, zr, bs, br, as_, ar, s0s, s0r, p1s, p1r,
-    q0s, q0r, q1s, q1r, q2s, q2r, r0s, r0r, r1s, r1r, r2s, r2r, es, er,
-    s1, t1, s2, t2, s3, t3, s4, t4, os_,
+    ls, hs, hr, h2r, ps, zs, bs, as_, ar, fs, q0r, q1r, q2r, r0r, r1r, r2r, rs, es, er, ts, os_,
 ):
     x, y, z, core = place()
     dp = lax.axis_index("dp")
@@ -255,86 +253,77 @@
         def _():
             greet(barrier, peer)
 
-    loads = []
     for cb in range(8):
         lanes = pl.ds(128 * cb, 128)
-        loads.append(pltpu.make_async_copy(field.at[:, :, lanes], fb.at[cb], ls.at[0, cb]))
-        loads.append(pltpu.make_async_copy(cot.at[:, lanes], cb_.at[cb], ls.at[1, cb]))
-    for copy in loads:
-        copy.start()
+        pltpu.make_async_copy(field.at[:, :, lanes], fb.at[cb], ls.at[0]).start()
+        pltpu.make_async_copy(cot.at[:, lanes], cb_.at[cb], ls.at[1]).start()
+
+    def settle(ref, sem):
+        pltpu.make_async_copy(ref, ref, sem).wait()
+
+    rows_in, rows_out = w_in[...].astype(F32), w_out[...].astype(F32)
+    raw[0, 0:4, :], raw[0, 4:8, :] = rows_in[0:4], rows_out[0:4]
+    raw[1, 0:2, :], raw[1, 2:4, :] = rows_in[4:6], rows_out[4:6]
+    raw[1, 4:8, :] = jnp.zeros((4, 1024), F32)
+    rawz[...] = raw[0].astype(BF16)
+    rawy[...] = raw[1].astype(BF16)
+    bia[...] = jnp.zeros((1, 128), F32)
+    bia[:, 0:6] = hbias[...].astype(F32)
+    slab[...] = jnp.zeros_like(slab)
+    slab[0:49, 0:64] = taps_in[...]
+    for k, v in enumerate((v0, v1, v2, v3, v4)):
+        slab[49 + k : 50 + k, 0:64] = v[...]
+    par[...] = jnp.where(lane < 64, slab[0:28, :], pltpu.roll(slab[28:56, :], 64, 1))
+    stage[...] = jnp.zeros_like(stage)
     halo1 = Halo(fb, ecol, ecor, hrows, hcols, hcors, hs, hr)
-    for copy in loads:
-        copy.wait()
     pl.semaphore_wait(barrier, 31 + 7 + 4 + halo_count())
 
-    zero = []
-    for k in range(1, NZ):
-        zero.append(remote(wt.at[turned(z, k, NZ)], rz.at[z], s0s.at[0, k - 1], s0r.at[0, k - 1], zps[k - 1]))
-    for k in range(1, NY):
-        zero.append(remote(wt.at[turned(y, k, NY)], ry.at[y], s0s.at[1, k - 1], s0r.at[1, k - 1], yps[k - 1]))
-    for copy in zero:
-        copy.start()
-    zcp = [remote(bia, zbias.at[z], zs.at[k], zr.at[k], peer) for k, peer in enumerate(zps)]
-    for copy in zcp:
-        copy.start()
-    pcp = [remote(par, pars.at[dp], ps.at[k], pr.at[k], peer) for k, peer in enumerate(dps)]
-    for copy in pcp:
-        copy.start()
-    rz[z] = wt[z]
-    ry[y] = wt[y]
+    for peer in zps:
+        remote(rawz, rz.at[z], fs.at[0], fs.at[1], peer).start()
+    for peer in yps:
+        remote(rawy, ry.at[y], fs.at[2], fs.at[3], peer).start()
+    for peer in zps:
+        remote(bia, zbias.at[z], zs.at[0], zs.at[1], peer).start()
+    settle(fb, ls.at[0])
+    settle(cb_, ls.at[1])
+    each(8, lambda cb: halo1.cut(cb, fb[cb].astype(F32), stage))
+    halo1.start()
+    for peer in dps:
+        remote(par, pars.at[dp], ps.at[0], ps.at[1], peer).start()
+    rz[z] = rawz[...]
+    ry[y] = rawy[...]
     zbias[z] = bia[...]
     pars[dp] = par[...]
-    stage[...] = jnp.zeros_like(stage)
-    each(8, lambda cb: halo1.cut(cb, fb[cb].astype(F32), stage))
-    halo1.start()
-
-    for copy in zero:
-        copy.wait()
-    home = (g0.at[y, x, z], g1.at[x, z, y], g2.at[z, y, x])
-    for k in range(3):
-        src = (rz, ry, ry)[k]
-        for d in range(8):
-            val = src[d].astype(F32)
-            scr[k, 0, 2 * d : 2 * d + 2, :] = val[2 * k : 2 * k + 2]
-            scr[k, 1, 2 * d : 2 * d + 2, :] = val[6 + 2 * k : 8 + 2 * k]
-        home[k][...] = scr[k].astype(BF16)
-    first = []
-    for k, peers in enumerate((zps, yps, xps)):
-        line = [remote(home[k], home[k], p1s.at[k, i], p1r.at[k, i], peer) for i, peer in enumerate(peers)]
-        for copy in line:
-            copy.start()
-        first.append(line)
-
-    for copy in zcp:
-        copy.wait()
-    total = zbias[0]
-    for k in range(1, NZ):
-        total = total + pltpu.roll(zbias[k], 6 * k, 1)
-    row[...] = total
-    me = x * 8 + y
-    bias[me] = total
-    bcp = [remote(row, bias.at[me], bs.at[k], br.at[k], peer) for k, peer in enumerate(xys)]
-    for copy in bcp:
-        copy.start()
+
+    to = lax.broadcasted_iota(jnp.int32, (32, 64), 0)
+    fro = lax.broadcasted_iota(jnp.int32, (32, 64), 1)
+
+    def tiles(got, first_row, step):
+        chosen = fro == ((to >> 1) & 7) * 8 + (to >> 4) * step + first_row + (to & 1)
+        rows = jnp.concatenate([got[d].astype(F32) for d in range(8)], axis=0).astype(BF16)
+        made = jnp.dot(jnp.where(chosen, 1.0, 0.0).astype(BF16), rows, preferred_element_type=F32)
+        return made.astype(BF16)
+
+    def put(home, made):
+        for cb in range(8):
+            for m in range(2):
+                home[cb, m] = made[16 * m : 16 * m + 16, 128 * cb : 128 * cb + 128]
 
     xr, xb = xps[0], xps[-1]
     yr, yb = yps[0], yps[-1]
     zr_, zb = zps[0], zps[-1]
     inner = [
-        Ring(4, 2, OFF4, lambda b, j: g0.at[y, turned(x, b, 4), pl.ds(4 * j, 4)], (xr, xb), q0s, q0r, 0.7),
-        Ring(8, 2, OFF8, lambda b, j: g1.at[x, turned(z, b, 8), pl.ds(4 * j, 4)], (zr_, zb), q1s, q1r, 0.7),
-        Ring(8, 2, OFF8, lambda b, j: g2.at[z, turned(y, b, 8), pl.ds(2 * j, 2)], (yr, yb), q2s, q2r, 0.35),
+        Ring(4, 2, OFF4, lambda b, j: g0.at[y, turned(x, b, 4), pl.ds(4 * j, 4)], (xr, xb), rs.at[0], q0r, 0.7),
+        Ring(8, 2, OFF8, lambda b, j: g1.at[x, turned(y, b, 8), pl.ds(4 * j, 4)], (yr, yb), rs.at[1], q1r, 0.7),
+        Ring(4, 2, OFF4, lambda b, j: g2.at[z, turned(x, b, 4), pl.ds(4 * j, 4)], (xr, xb), rs.at[2], q2r, 0.7),
     ]
     outer = [
-        Ring(8, 4, OFF4, lambda b, j: g0.at[turned(y, b, 8), turned(x, OFF4[j], 4)], (yr, yb), r0s, r0r, 1.4),
-        Ring(4, 8, OFF8, lambda b, j: g1.at[turned(x, b, 4), turned(z, OFF8[j], 8)], (xr, xb), r1s, r1r, 1.4),
-        Ring(8, 8, OFF8, lambda b, j: g2.at[turned(z, b, 8), turned(y, OFF8[j], 8)], (zr_, zb), r2s, r2r, 0.7),
+        Ring(8, 4, OFF4, lambda b, j: g0.at[turned(y, b, 8), turned(x, OFF4[j], 4)], (yr, yb), rs.at[3], r0r, 1.4),
+        Ring(4, 8, OFF8, lambda b, j: g1.at[turned(x, b, 4), turned(y, OFF8[j], 8)], (xr, xb), rs.at[4], r1r, 1.4),
+        Ring(8, 4, OFF4, lambda b, j: g2.at[turned(z, b, 8), turned(x, OFF4[j], 4)], (zr_, zb), rs.at[5], r2r, 1.4),
     ]
-    started = []
-
     def go(copy):
         copy.start()
-        started.append(copy)
 
     def arrive(k, level, way, s, j):
         ring = (inner, outer)[level][k]
@@ -350,9 +339,21 @@
 
     ship = [remote(act.at[a, core], act.at[a, core], as_.at[a], ar.at[a], sibling) for a in range(2)]
 
+    def bias_push():
+        settle(zbias.at[0:7], zs.at[0])
+        settle(zbias.at[0:7], zs.at[1])
+        total = zbias[0]
+        for k in range(1, NZ):
+            total = total + pltpu.roll(zbias[k], 6 * k, 1)
+        row[...] = total
+        me = x * 8 + y
+        bias[me] = total
+        for peer in xys:
+            remote(row, bias.at[me], bs.at[0], bs.at[1], peer).start()
+
     def params():
-        for copy in pcp:
-            copy.wait()
+        settle(pars.at[0:15], ps.at[0])
+        settle(pars.at[0:15], ps.at[1])
 
         def unpack(cb):
             one, two = pars[2 * cb], pars[2 * cb + 1]
@@ -393,8 +394,8 @@
 
     def biases():
         ship[0].start()
-        for copy in bcp:
-            copy.wait()
+        settle(bias.at[0:31], bs.at[0])
+        settle(bias.at[0:31], bs.at[1])
         values = bias[...].reshape(32, 128).astype(BF16)
         j = lax.broadcasted_iota(jnp.int32, (128, 128), 0)
         l = lax.broadcasted_iota(jnp.int32, (128, 128), 1)
@@ -409,8 +410,8 @@
 
         t0 = pick(j == 6 * ((l >> 1) & 7) + (l & 1))
         table[0] = jnp.sum(jnp.where(bx == (l64 >> 4), t0, 0.0), axis=0)
-        t1_ = pick(j == 6 * (l >> 4) + 2 + (l & 1))
-        table[1, 0:4, :] = jnp.sum(jnp.where(by == ((bl >> 1) & 7), t1_, 0.0), axis=1)
+        t1_ = pick(j == 6 * ((l >> 1) & 7) + 2 + (l & 1))
+        table[1, 0:4, :] = jnp.sum(jnp.where(by == (bl >> 4), t1_, 0.0), axis=1)
         for zz in range(8):
             t2_ = pick(j == 6 * zz + 4 + (l & 1))
             kept = jnp.where((bx == (l64 >> 4)) & (by == ((bl >> 1) & 7)), t2_, 0.0)
@@ -431,7 +432,7 @@
                 elif k == 1:
                     pieces.append(g1[at[1](off), :, cb, m].reshape(128, 128))
                 else:
-                    pieces.append(g2[at[2](off), cb, :, m].reshape(64, 128))
+                    pieces.append(g2[at[2](off), :, cb, m].reshape(64, 128))
             columns.append(jnp.concatenate(pieces, axis=0))
         return jnp.concatenate(columns, axis=1)
 
@@ -466,16 +467,18 @@
                 piece = value[:, :, 128 * cb : 128 * cb + 128]
                 acc[m, :, cb] = piece if n == 0 else acc[m, :, cb] + piece
 
-    tasks = [(0.7, None, functools.partial(conv_piece, i)) for i in range(4)]
-    tasks += [(1.0, None, norm), (0.8, None, biases)]
+    tasks = [(0.3, 0.5, None, bias_push), (0.6, 1.5, None, params), (1.2, 2.5, None, borders)]
+    tasks += [(0.6, 0.0, None, functools.partial(conv_piece, i)) for i in range(4)]
+    tasks += [(0.8, 0.0, None, norm), (0.6, 0.0, None, biases)]
     for n in range(LAST):
-        tasks.append((1.2, CHUNKS[n], functools.partial(chunk_front, n)))
-        tasks.append((1.0, CHUNKS[n], functools.partial(chunk_back, n)))
-    params()
-    borders()
-    for k in range(3):
-        for copy in first[k]:
-            copy.wait()
+        tasks.append((1.0, 0.0, CHUNKS[n], functools.partial(chunk_front, n)))
+        tasks.append((0.8, 0.0, CHUNKS[n], functools.partial(chunk_back, n)))
+    home = (g0.at[y, x], g1.at[x, y], g2.at[z, x])
+    for k, (got, first_row, step) in enumerate(((rz, 0, 4), (rz, 2, 4), (ry, 0, 2))):
+        if k != 1:
+            settle((rz, ry)[k // 2].at[0:7], fs.at[k])
+            settle((rz, ry)[k // 2].at[0:7], fs.at[k + 1])
+        put(home[k], tiles(got, first_row, step))
         for way in (0, 1):
             go(outer[k].copy(way, 1, 0))
             for j in range(2):
@@ -497,13 +500,13 @@
 
     clock = 0.0
     while events or tasks:
-        ready = bool(tasks) and not any(needs(e, tasks[0][1]) for e in events)
-        if events and (events[0][0] <= clock or not ready):
+        ready = bool(tasks) and not any(needs(e, tasks[0][2]) for e in events)
+        if events and (events[0][0] <= clock or not ready or clock < tasks[0][1]):
             event = events.pop(0)
             clock = max(clock, event[0])
             arrive(*event[1:])
         else:
-            length, _, piece = tasks.pop(0)
+            length, _, _, piece = tasks.pop(0)
             piece()
             clock += length
 
@@ -549,7 +552,7 @@
     one, two = lax.fori_loop(0, 8, ending, (none, none))
     mean_one = jnp.sum(one, axis=-1, keepdims=True) * (1.0 / 1024)
     mean_two = jnp.sum(two, axis=-1, keepdims=True) * (1.0 / 1024)
-    halo2 = Halo(wire, ecol, ecor, wrows, wcols, wcors, h2s, h2r)
+    halo2 = Halo(wire, ecol, ecor, wrows, wcols, wcors, hs, h2r)
     inverse = inv[...]
 
     def rear(cb):
@@ -562,10 +565,8 @@
 
     each(8, rear)
     halo2.start()
-    puts = []
     for cb in range(8):
-        puts.append(pltpu.make_async_copy(ob.at[0, cb], block_out.at[:, pl.ds(128 * cb, 128)], os_.at[0, cb]))
-        puts[-1].start()
+        pltpu.make_async_copy(ob.at[0, cb], block_out.at[:, pl.ds(128 * cb, 128)], os_.at[0]).start()
 
     def block_grad(cb):
         back = bc[cb].reshape(8, 16, 128)
@@ -578,7 +579,7 @@
     def firsts(k):
         other = lax.rem(mine + k, 8)
         peer = device(lax.rem(other, 2) * 2 + xl, yh * 4 + lax.div(other, 2), z, core)
-        return other, remote(sums.at[other], r1.at[mine], s1.at[k - 1], t1.at[k - 1], peer)
+        return other, remote(sums.at[other], r1.at[mine], ts.at[0], ts.at[1], peer)
 
     def grad_step(i):
         other, copy = firsts(i + 1)
@@ -599,81 +600,77 @@
 
         each(count, one)
         for cb in range(low_, low_ + count):
-            puts.append(pltpu.make_async_copy(ob.at[1, cb], grad_in.at[:, pl.ds(128 * cb, 128)], os_.at[1, cb]))
-            puts[-1].start()
+            pltpu.make_async_copy(ob.at[1, cb], grad_in.at[:, pl.ds(128 * cb, 128)], os_.at[1]).start()
 
     conv_back(0, 2)
-    for k in range(1, 8):
-        firsts(k)[1].wait()
+    settle(r1.at[0:7], ts.at[0])
+    settle(r1.at[0:7], ts.at[1])
     mid[...] = jnp.sum(r1[...], axis=0).reshape(8, 8, 128)
-    c2 = [remote(mid.at[turned(z, k + 1, 8)], r2.at[z], s2.at[k], t2.at[k], zps[k]) for k in range(7)]
-    for copy in c2:
-        copy.start()
+    for k in range(7):
+        remote(mid.at[turned(z, k + 1, 8)], r2.at[z], ts.at[2], ts.at[3], zps[k]).start()
     r2[z] = mid[z]
     conv_back(2, 3)
-    for copy in c2:
-        copy.wait()
+    settle(r2.at[0:7], ts.at[3])
     low[...] = jnp.sum(r2[...], axis=0)
-    c3 = [remote(low, r3.at[member], s3.at[k], t3.at[k], thirds[k]) for k in range(7)]
-    for copy in c3:
-        copy.start()
+    for k in range(7):
+        remote(low, r3.at[member], ts.at[4], ts.at[5], thirds[k]).start()
     r3[member] = low[...]
     conv_back(5, 3)
-    for copy in c3:
-        copy.wait()
+    settle(r3.at[0:7], ts.at[5])
     fin[...] = jnp.sum(r3[...], axis=0)
-    c4 = [remote(fin, tot.at[z], s4.at[k], t4.at[k], zps[k]) for k in range(7)]
-    for copy in c4:
-        copy.start()
+    for k in range(7):
+        remote(fin, tot.at[z], ts.at[6], ts.at[7], zps[k]).start()
     tot[z] = fin[...]
-    for copy in started + swap:
+    for k, ref in enumerate((g0.at[0, 0:3], g1.at[0, 0:7], g2.at[0, 0:3], g0.at[0:7], g1.at[0:3], g2.at[0:7])):
+        settle(ref, rs.at[k])
+    for copy in swap:
         copy.wait_send()
-    for copy in puts:
-        copy.wait()
-    for copy in c4:
-        copy.wait()
+    settle(r2.at[0:7], ts.at[2])
+    settle(r3.at[0:7], ts.at[4])
+    settle(ob.at[0], os_.at[0])
+    settle(ob.at[1], os_.at[1])
+    settle(tot.at[0:7], ts.at[6])
+    settle(tot.at[0:7], ts.at[7])
     final = tot[...].reshape(64, 128) * (1.0 / 256.0)
     final = jnp.where(xl == 0, final, pltpu.roll(final, 64, 1))
-    out_kernel[...] = final[0:49, 0:64]
-    out_vec[...] = final[48:56, 0:64]
-
-
-def whole(field, cot, wt, par, bia):
+    out_sums[...] = final[0:56, 0:64]
+
+
+def whole(*args):
     cell = (2, 16, 128)
     any_ = pl.BlockSpec(memory_space=pl.ANY)
     scratch = [
-        ((8, 8, 16, 128), BF16), ((8, 128, 128), BF16), ((2, 8, 24, 128), BF16), ((4, 8, 16, 128), BF16), ((112, 128), F32),
+        ((8, 8, 16, 128), BF16), ((8, 128, 128), BF16), ((2, 8, 1024), F32), ((8, 1024), BF16), ((8, 1024), BF16),
+        ((56, 128), F32), ((28, 128), F32), ((1, 128), F32), ((2, 8, 24, 128), BF16), ((4, 8, 16, 128), BF16), ((112, 128), F32),
         ((2, 8, 3, 16, 128), BF16), ((2, 8, 24, 128), BF16), ((4, 8, 16, 128), BF16),
         ((2, 8, 3, 16, 128), BF16), ((2, 8, 24, 128), BF16), ((4, 8, 16, 128), BF16),
         ((8, 14, 32, 128), F32), ((8, 14, 32, 128), F32), ((16, 28, 128), F32), ((8, 56, 128), F32),
         ((1, 128), F32), ((8, 1, 128), F32), ((32, 1, 128), F32), ((3, 8, 128), F32),
-        ((8, 16, 128), BF16), ((8, 16, 128), BF16), ((3, 2, 16, 128), F32),
-        ((8, 4, 8) + cell, BF16), ((4, 8, 8) + cell, BF16), ((8, 8, 4) + cell, BF16),
+        ((8, 8, 1024), BF16), ((8, 8, 1024), BF16),
+        ((8, 4, 8) + cell, BF16), ((4, 8, 8) + cell, BF16), ((8, 4, 8) + cell, BF16),
         ((2, 2, 128, 1024), BF16), ((2, 256, 256), BF16), ((2, 2, 8, 128, 128), F32),
         ((2, 8, 128, 128), BF16), ((2, 8, 128, 128), BF16), ((8, 128, 128), F32), ((128, 128), F32),
         ((8, 128, 128), F32), ((8, 8, 16, 128), BF16), ((2, 8, 128, 128), BF16), ((8, 64, 128), F32),
         ((8, 64, 128), F32), ((8, 8, 128), F32), ((8, 8, 128), F32), ((8, 8, 128), F32), ((8, 128), F32), ((8, 128), F32),
         ((8, 8, 128), F32),
     ]
-    sems = [(2, 8), (8,), (8,), (8,), (8,), (15,), (15,), (7,), (7,), (31,), (31,), (2,), (2,), (2, 7), (2, 7), (3, 7), (3, 7)]
-    sems += [(2, 3), (2, 3), (2, 7), (2, 7), (2, 7), (2, 7), (2, 14), (2, 14), (2, 12), (2, 12), (2, 28), (2, 28), (2,), (2,)]
-    sems += [(7,)] * 8 + [(2, 8)]
+    sems = [(2,), (8,), (8,), (8,), (2,), (2,), (2,), (2,), (2,), (4,), (2, 3), (2, 7), (2, 3), (2, 14), (2, 12), (2, 14)]
+    sems += [(6,), (2,), (2,), (8,), (2,)]
     return pl.pallas_call(
         whole_body,
         out_shape=(
             jax.ShapeDtypeStruct((128, 1024), BF16),
             jax.ShapeDtypeStruct((128, 1024), BF16),
-            jax.ShapeDtypeStruct((49, 64), F32),
-            jax.ShapeDtypeStruct((8, 64), F32),
+            jax.ShapeDtypeStruct((56, 64), F32),
         ),
-        in_specs=[any_, any_, VMEM, VMEM, VMEM],
-        out_specs=[any_, any_, VMEM, VMEM],
+        in_specs=[any_, any_] + [VMEM] * 9,
+        out_specs=[any_, any_, VMEM],
         scratch_shapes=[pltpu.VMEM(*s) for s in scratch] + [DMA(s) for s in sems],
         compiler_params=pltpu.CompilerParams(
             collective_id=0, has_side_effects=True, vmem_limit_bytes=56 * 1024 * 1024
         ),
         name="whole",
-    )(field, cot, wt, par, bia)
+    )(*args)
 
 
 def per_device(
@@ -692,22 +689,16 @@
     _, _, rows, cols, width = features.shape
     field = features.reshape(rows, cols, width)
     cot = cotangent.reshape(rows * cols, width)
-    slab = jnp.concatenate(
-        [kernel] + [v[None] for v in (conv_bias, norm_gain, norm_bias, layer_scale, out_bias)] + [jnp.zeros((2, 64), F32)]
-    )
-    par = jnp.concatenate([slab[:28], slab[28:]], axis=1)
-    bia = jnp.pad(hidden_bias.astype(F32)[None], ((0, 0), (0, 122)))
-    both = jnp.concatenate([in_weight, out_weight, jnp.zeros((4, width), BF16)])
-    wt = both.reshape(16, 8, 128).transpose(1, 0, 2)
-    block_out, grad_in, out_kernel, out_vec = whole(field, cot, wt, par, bia)
+    vectors = [v.reshape(1, -1) for v in (conv_bias, norm_gain, norm_bias, layer_scale, out_bias)]
+    block_out, grad_in, sums = whole(field, cot, in_weight, out_weight, hidden_bias.reshape(1, -1), kernel, *vectors)
     return (
         block_out.reshape(features.shape),
         grad_in.reshape(features.shape),
-        out_kernel,
-        out_vec[1],
-        out_vec[2],
-        out_vec[3],
-        out_vec[4],
+        sums[0:49],
+        sums[49],
+        sums[50],
+        sums[51],
+        sums[52],
     )
 
 

time: 115 us -> 102 us (0.89)
  Pallas kernels: 105 us -> 96.6 us
  local copies, waits for them, and re-layouts: 7.33 us -> 4.42 us
  other arithmetic: 1.88 us -> 0 us
    pallas_call x1, Pallas kernels: 105 us -> 96.6 us  [whole(): pl.pallas_call(whole_body, out_shape=(jax.ShapeDtypeStruct((128, 1024), B...]
    unnamed x23 -> x7, local copies, waits for them, and re-layouts: 4.4 us -> 3.07 us
where the time goes in v3:
time: 102 us
  Pallas kernels  96.6 us (95%)
  local copies, waits for them, and re-layouts  4.42 us (4%)
    pallas_call x1, Pallas kernels, whole(): pl.pallas_call(whole_body, out_shape=(jax.ShapeDtypeStruct((128, 1024), B...  96.6 us
    unnamed x7, local copies, waits for them, and re-layouts  3.07 us

profile of v3, /device:TPU:8, one launch (start us, length us, event | category | flops | bytes accessed | tf_op | source)
XLA Modules:
  0.0 101.6 jit_solution(1128633657036291617)
XLA Ops:
  0.6 96.6 %whole.1 = (bf16[128,1024]{1,0:T(8,128)(2,1)}, bf16[128,1024]{1,0:T(8,128)(2,1)}, f32[56,64]{1,0:T(8,128)}) custom-call(bf16[8,16,1024]{2,1,0:T(8,128)(2,1)} %bitcast.19, bf16[128,1024]{1,0:T(8,128)(2,1)} %bitcast.20, bf16[6,1024]{1,0:T(8,128)(2,1)} %w_in.1, bf16[6,1024]{1,0:T(8,128)(2,1)} %w_out.1, bf16[1,6]{1,0:T(2,128)(2,1)} %bitcast.24, ...), custom_call_target="tpu_custom_call" | custom-call | tf_op jit(solution)/shard_map/whole/pallas_call | solution.py:659
  97.2 1.3 %slice_bitcast_fusion = (f32[64]{0:T(128)}, f32[64]{0:T(128)}, f32[64]{0:T(128)}, f32[64]{0:T(128)}) fusion(f32[56,64]{1,0:T(8,128)} %get-tuple-element.12), kind=kLoop, calls=%fused_computation | loop fusion | bytes 2048 | tf_op jit(solution)/shard_map/squeeze | solution.py:701
  98.6 0.0 copy-start
  98.6 1.7 %copy.21 = bf16[1,1,8,16,1024]{4,3,2,1,0:T(8,128)(2,1)} copy(bf16[1,1,8,16,1024]{4,3,2,1,0:T(8,128)(2,1)} %bitcast.22) | data formatting | bytes 524288
  100.3 0.0 copy-done
  100.3 0.0 copy-start.1
  100.3 0.7 copy.22
  101.0 0.0 copy-done.1
  101.0 0.6 copy.23
Async XLA Ops:
  98.6 1.7 %copy-start = (bf16[128,1024]{1,0:T(8,128)(2,1)S(1)}, bf16[128,1024]{1,0:T(8,128)(2,1)}, u32[]{:S(2)}) copy-start(bf16[128,1024]{1,0:T(8,128)(2,1)} %get-tuple-element.11) | copy-start | bytes 786436
  100.3 0.7 copy-start.1

commit v4 on v3

--- a/solution.py
+++ b/solution.py
@@ -1,4 +1,5 @@
 import functools
+import heapq
 
 import jax
 import jax.numpy as jnp
@@ -76,8 +77,8 @@
 
 
 class Ring:
-    def __init__(self, n, count, offs, sub, peers, ssem, rsem, wire):
-        self.n, self.count, self.offs, self.sub, self.peers = n, count, offs, sub, peers
+    def __init__(self, axis, n, count, offs, sub, peers, ssem, rsem, wire):
+        self.axis, self.n, self.count, self.offs, self.sub, self.peers = axis, n, count, offs, sub, peers
         self.ssem, self.rsem, self.wire = ssem, rsem, wire
         self.slots = ring_slots(n, count)
 
@@ -91,37 +92,49 @@
         ref = self.sub(-s if way == 0 else s, j)
         return pltpu.make_async_copy(ref, ref, self.rsem.at[way, i])
 
-
-def plan(outer, inner):
-    events = []
-    latency = 1.7
-    for c, (o, i) in enumerate(zip(outer, inner)):
-        ready = {0: 0.0}
+    def completes(self, way, s, seen):
+        half = self.n // 2
+        parts = [(w, s, j) for w in (0, 1) for j in range(self.count) if (s, j) in self.slots[w] and (s == half or w == way)]
+        if not all(part in seen for part in parts):
+            return None
+        return self.offs.index(half if s == half else -s if way == 0 else s)
+
+
+def plan(outer, inner, begin):
+    rings = (inner, outer)
+    free = {(axis, way): late for axis, late in zip("xyz", (0.0, 1.0, 2.0)) for way in (0, 1)}
+    heap, events, seen = [], [], {}
+    count = 0
+
+    def push(at, what):
+        nonlocal count
+        count += 1
+        heapq.heappush(heap, (at, count, what))
+
+    for k in range(3):
         for way in (0, 1):
-            t, got = 0.0, {}
-            for s, j in i.slots[way]:
-                t = max(t, 0.0 if s == 1 else got[s - 1, j]) + i.wire
-                got[s, j] = t + latency
-                events.append((got[s, j], c, 0, way, s, j))
+            for j in range(2):
+                push(begin[k], (False, k, 0, way, 1, j))
         for way in (0, 1):
-            for s, j in i.slots[way]:
-                pass
-        half = i.n // 2
-        seen = {(e[3], e[4], e[5]): e[0] for e in events if e[1] == c and e[2] == 0}
-        for k, off in enumerate(o.offs):
-            if off == 0:
-                continue
-            if abs(off) == half:
-                ready[k] = max(v for (w, s, j), v in seen.items() if s == half)
-            else:
-                ready[k] = max(v for (w, s, j), v in seen.items() if s == abs(off) and w == (0 if off < 0 else 1))
-        for way in (0, 1):
-            t, got = 0.0, {}
-            for s, j in o.slots[way]:
-                t = max(t, ready[j] if s == 1 else got[s - 1, j]) + o.wire
-                got[s, j] = t + latency
-                events.append((got[s, j], c, 1, way, s, j))
-    return sorted(events)
+            push(begin[k], (False, k, 1, way, 1, 0))
+    while heap:
+        at, _, (arrived, k, level, way, s, j) = heapq.heappop(heap)
+        ring = rings[level][k]
+        if not arrived:
+            end = max(at, free[ring.axis, way]) + ring.wire
+            free[ring.axis, way] = end
+            push(end + 1.7, (True, k, level, way, s, j))
+            continue
+        events.append((at, k, level, way, s, j))
+        if (s + 1, j) in ring.slots[way]:
+            push(at, (False, k, level, way, s + 1, j))
+        if level == 0:
+            seen.setdefault(k, set()).add((way, s, j))
+            index = ring.completes(way, s, seen[k])
+            for w in (0, 1):
+                if index is not None and (1, index) in outer[k].slots[w]:
+                    push(at, (False, k, 1, w, 1, index))
+    return events
 
 
 def halo_count():
@@ -313,28 +326,30 @@
     yr, yb = yps[0], yps[-1]
     zr_, zb = zps[0], zps[-1]
     inner = [
-        Ring(4, 2, OFF4, lambda b, j: g0.at[y, turned(x, b, 4), pl.ds(4 * j, 4)], (xr, xb), rs.at[0], q0r, 0.7),
-        Ring(8, 2, OFF8, lambda b, j: g1.at[x, turned(y, b, 8), pl.ds(4 * j, 4)], (yr, yb), rs.at[1], q1r, 0.7),
-        Ring(4, 2, OFF4, lambda b, j: g2.at[z, turned(x, b, 4), pl.ds(4 * j, 4)], (xr, xb), rs.at[2], q2r, 0.7),
+        Ring("x", 4, 2, OFF4, lambda b, j: g0.at[y, turned(x, b, 4), pl.ds(4 * j, 4)], (xr, xb), rs.at[0], q0r, 0.7),
+        Ring("y", 8, 2, OFF8, lambda b, j: g1.at[x, turned(y, b, 8), pl.ds(4 * j, 4)], (yr, yb), rs.at[1], q1r, 0.7),
+        Ring("x", 4, 2, OFF4, lambda b, j: g2.at[z, turned(x, b, 4), pl.ds(4 * j, 4)], (xr, xb), rs.at[2], q2r, 0.7),
     ]
     outer = [
-        Ring(8, 4, OFF4, lambda b, j: g0.at[turned(y, b, 8), turned(x, OFF4[j], 4)], (yr, yb), rs.at[3], r0r, 1.4),
-        Ring(4, 8, OFF8, lambda b, j: g1.at[turned(x, b, 4), turned(y, OFF8[j], 8)], (xr, xb), rs.at[4], r1r, 1.4),
-        Ring(8, 4, OFF4, lambda b, j: g2.at[turned(z, b, 8), turned(x, OFF4[j], 4)], (zr_, zb), rs.at[5], r2r, 1.4),
+        Ring("y", 8, 4, OFF4, lambda b, j: g0.at[turned(y, b, 8), turned(x, OFF4[j], 4)], (yr, yb), rs.at[3], r0r, 1.4),
+        Ring("x", 4, 8, OFF8, lambda b, j: g1.at[turned(x, b, 4), turned(y, OFF8[j], 8)], (xr, xb), rs.at[4], r1r, 1.4),
+        Ring("z", 8, 4, OFF4, lambda b, j: g2.at[turned(z, b, 8), turned(x, OFF4[j], 4)], (zr_, zb), rs.at[5], r2r, 1.4),
     ]
     def go(copy):
         copy.start()
+
+    seen = [set(), set(), set()]
 
     def arrive(k, level, way, s, j):
         ring = (inner, outer)[level][k]
         ring.landed(way, s, j).wait()
         if (s + 1, j) in ring.slots[way]:
             go(ring.copy(way, s + 1, j))
-        half = ring.n // 2
-        if level == 0 and j == (1 if s < half else way) and not (s == half and way == 0):
-            index = ring.offs.index(half if s == half else -s if way == 0 else s)
+        if level == 0:
+            seen[k].add((way, s, j))
+            index = ring.completes(way, s, seen[k])
             for w in (0, 1):
-                if (1, index) in outer[k].slots[w]:
+                if index is not None and (1, index) in outer[k].slots[w]:
                     go(outer[k].copy(w, 1, index))
 
     ship = [remote(act.at[a, core], act.at[a, core], as_.at[a], ar.at[a], sibling) for a in range(2)]
@@ -480,10 +495,11 @@
             settle((rz, ry)[k // 2].at[0:7], fs.at[k + 1])
         put(home[k], tiles(got, first_row, step))
         for way in (0, 1):
-            go(outer[k].copy(way, 1, 0))
             for j in range(2):
                 go(inner[k].copy(way, 1, j))
-    events = plan(outer, inner)
+        for way in (0, 1):
+            go(outer[k].copy(way, 1, 0))
+    events = plan(outer, inner, (0.0, 0.3, 0.6))
 
     def needs(event, blocks):
         _, k, level, way, s, j = event
@@ -559,14 +575,7 @@
         back = inverse * (bc[cb] - mean_one - conv[cb] * mean_two)
         bc[cb] = back
         sums[cb, 49:50, :] = down(back)
-        back = back.reshape(8, 16, 128)
-        wire[cb] = back.astype(BF16)
-        halo2.cut(cb, back, stage)
-
-    each(8, rear)
-    halo2.start()
-    for cb in range(8):
-        pltpu.make_async_copy(ob.at[0, cb], block_out.at[:, pl.ds(128 * cb, 128)], os_.at[0]).start()
+        wire[cb] = back.reshape(8, 16, 128).astype(BF16)
 
     def block_grad(cb):
         back = bc[cb].reshape(8, 16, 128)
@@ -583,13 +592,18 @@
 
     def grad_step(i):
         other, copy = firsts(i + 1)
+        rear(other)
         block_grad(other)
         copy.start()
 
     each(7, grad_step)
+    rear(mine)
     block_grad(mine)
     r1[mine] = sums[mine]
-    halo2.finish()
+    each(8, lambda cb: halo2.cut(cb, bc[cb].reshape(8, 16, 128), stage))
+    halo2.start()
+    for cb in range(8):
+        pltpu.make_async_copy(ob.at[0, cb], block_out.at[:, pl.ds(128 * cb, 128)], os_.at[0]).start()
 
     def conv_back(low_, count):
         def one(i):
@@ -602,25 +616,26 @@
         for cb in range(low_, low_ + count):
             pltpu.make_async_copy(ob.at[1, cb], grad_in.at[:, pl.ds(128 * cb, 128)], os_.at[1]).start()
 
-    conv_back(0, 2)
-    settle(r1.at[0:7], ts.at[0])
     settle(r1.at[0:7], ts.at[1])
     mid[...] = jnp.sum(r1[...], axis=0).reshape(8, 8, 128)
     for k in range(7):
         remote(mid.at[turned(z, k + 1, 8)], r2.at[z], ts.at[2], ts.at[3], zps[k]).start()
     r2[z] = mid[z]
-    conv_back(2, 3)
+    halo2.finish()
+    conv_back(0, 3)
     settle(r2.at[0:7], ts.at[3])
     low[...] = jnp.sum(r2[...], axis=0)
     for k in range(7):
         remote(low, r3.at[member], ts.at[4], ts.at[5], thirds[k]).start()
     r3[member] = low[...]
-    conv_back(5, 3)
+    conv_back(3, 3)
     settle(r3.at[0:7], ts.at[5])
     fin[...] = jnp.sum(r3[...], axis=0)
     for k in range(7):
         remote(fin, tot.at[z], ts.at[6], ts.at[7], zps[k]).start()
     tot[z] = fin[...]
+    conv_back(6, 2)
+    settle(r1.at[0:7], ts.at[0])
     for k, ref in enumerate((g0.at[0, 0:3], g1.at[0, 0:7], g2.at[0, 0:3], g0.at[0:7], g1.at[0:3], g2.at[0:7])):
         settle(ref, rs.at[k])
     for copy in swap:
@@ -673,6 +688,14 @@
     )(*args)
 
 
+def hand_out(block_in, grad_in, sums, block_out, grad_out, kernel_out, *rest):
+    block_out[...] = block_in[...]
+    grad_out[...] = grad_in[...]
+    kernel_out[...] = sums[0:49, :]
+    for k, out in enumerate(rest):
+        out[...] = sums[49 + k : 50 + k, :]
+
+
 def per_device(
     features,
     cotangent,
@@ -689,17 +712,19 @@
     _, _, rows, cols, width = features.shape
     field = features.reshape(rows, cols, width)
     cot = cotangent.reshape(rows * cols, width)
+    pixels = rows * cols
     vectors = [v.reshape(1, -1) for v in (conv_bias, norm_gain, norm_bias, layer_scale, out_bias)]
-    block_out, grad_in, sums = whole(field, cot, in_weight, out_weight, hidden_bias.reshape(1, -1), kernel, *vectors)
-    return (
-        block_out.reshape(features.shape),
-        grad_in.reshape(features.shape),
-        sums[0:49],
-        sums[49],
-        sums[50],
-        sums[51],
-        sums[52],
-    )
+    made = whole(field, cot, in_weight, out_weight, hidden_bias.reshape(1, -1), kernel, *vectors)
+    block_out, grad_in, out_kernel, *rest = pl.pallas_call(
+        hand_out,
+        out_shape=[jax.ShapeDtypeStruct((pixels, width), BF16)] * 2
+        + [jax.ShapeDtypeStruct((49, 64), F32)]
+        + [jax.ShapeDtypeStruct((1, 64), F32)] * 4,
+        in_specs=[VMEM] * 3,
+        out_specs=[VMEM] * 7,
+        name="hand_out",
+    )(*made)
+    return (block_out.reshape(features.shape), grad_in.reshape(features.shape), out_kernel, *[v.reshape(-1) for v in rest])
 
 
 def solution(mesh):

time: 102 us -> 101 us (level)
  local copies, waits for them, and re-layouts: 4.42 us -> 0 us
  Pallas kernels: 96.6 us -> 100 us
    unnamed x7 -> x0, local copies, waits for them, and re-layouts: 3.07 us -> none
    pallas_call x0 -> x1, Pallas kernels: none -> 1.85 us  [per_device(): pl.pallas_call(hand_out, out_shape=[jax.ShapeDtypeStruct((pixels, width),...]
    pallas_call x1, Pallas kernels: 96.6 us -> 98.3 us  [whole(): pl.pallas_call(whole_body, out_shape=(jax.ShapeDtypeStruct((128, 1024), B...]
    squeeze x1 -> x0, local copies, waits for them, and re-layouts: 1.35 us -> none  [per_device(): sums[52]]
where the time goes in v4:
time: 101 us
  Pallas kernels  100 us (99%)
    pallas_call x1, Pallas kernels, whole(): pl.pallas_call(whole_body, out_shape=(jax.ShapeDtypeStruct((128, 1024), B...  98.3 us

profile of v4, /device:TPU:8, one launch (start us, length us, event | category | flops | bytes accessed | tf_op | source)
XLA Modules:
  0.0 100.8 jit_solution(12579966808625054452)
XLA Ops:
  0.6 98.3 %whole.1 = (bf16[128,1024]{1,0:T(8,128)(2,1)}, bf16[128,1024]{1,0:T(8,128)(2,1)}, f32[56,64]{1,0:T(8,128)}) custom-call(bf16[8,16,1024]{2,1,0:T(8,128)(2,1)} %bitcast.14, bf16[128,1024]{1,0:T(8,128)(2,1)} %bitcast.15, bf16[6,1024]{1,0:T(8,128)(2,1)} %w_in.1, bf16[6,1024]{1,0:T(8,128)(2,1)} %w_out.1, bf16[1,6]{1,0:T(2,128)(2,1)} %bitcast.16, ...), custom_call_target="tpu_custom_call" | custom-call | tf_op jit(solution)/shard_map/whole/pallas_call | solution.py:674
  99.0 1.9 %hand_out.1 = (bf16[128,1024]{1,0:T(8,128)(2,1)}, bf16[128,1024]{1,0:T(8,128)(2,1)}, f32[49,64]{1,0:T(8,128)}, f32[1,64]{1,0:T(1,128)}, f32[1,64]{1,0:T(1,128)}, /*index=5*/f32[1,64]{1,0:T(1,128)}, f32[1,64]{1,0:T(1,128)}) custom-call(bf16[128,1024]{1,0:T(8,128)(2,1)} %get-tuple-element.17.block_in, bf16[128,1024]{1,0:T(8,128)(2,1)} %get-tuple-element.18.grad_in, ...), custom_call_target="tpu_custom_call" | custom-call | tf_op jit(solution)/shard_map/hand_out/pallas_call | solution.py:718

commit v5 on v4

--- a/solution.py
+++ b/solution.py
@@ -100,41 +100,60 @@
         return self.offs.index(half if s == half else -s if way == 0 else s)
 
 
+LEAD = 1.5
+
+
 def plan(outer, inner, begin):
     rings = (inner, outer)
     free = {(axis, way): late for axis, late in zip("xyz", (0.0, 1.0, 2.0)) for way in (0, 1)}
-    heap, events, seen = [], [], {}
+    queues = {link: [] for link in free}
+    heap, steps, seen = [], [], {}
     count = 0
 
-    def push(at, what):
+    def push(at, kind, what):
         nonlocal count
         count += 1
-        heapq.heappush(heap, (at, count, what))
-
+        heapq.heappush(heap, (at, count, kind, what))
+
+    def dispatch(at, link):
+        if queues[link] and free[link] <= at:
+            _, _, ready, given, (k, level, way, s, j) = heapq.heappop(queues[link])
+            free[link] = at + rings[level][k].wire
+            push(free[link], "free", link)
+            push(free[link] + 1.7, "landed", (k, level, way, s, j))
+            if not given:
+                steps.append((max(ready, at - LEAD), 1, (k, level, way, s, j)))
+
+    for link, late in free.items():
+        push(late, "free", link)
     for k in range(3):
         for way in (0, 1):
             for j in range(2):
-                push(begin[k], (False, k, 0, way, 1, j))
+                push(begin[k], "given", (k, 0, way, 1, j))
         for way in (0, 1):
-            push(begin[k], (False, k, 1, way, 1, 0))
+            push(begin[k], "given", (k, 1, way, 1, 0))
     while heap:
-        at, _, (arrived, k, level, way, s, j) = heapq.heappop(heap)
+        at, number, kind, what = heapq.heappop(heap)
+        if kind == "free":
+            dispatch(at, what)
+            continue
+        k, level, way, s, j = what
         ring = rings[level][k]
-        if not arrived:
-            end = max(at, free[ring.axis, way]) + ring.wire
-            free[ring.axis, way] = end
-            push(end + 1.7, (True, k, level, way, s, j))
+        if kind in ("ready", "given"):
+            link = (ring.axis, way)
+            heapq.heappush(queues[link], (0 if kind == "given" else level, number, at, kind == "given", what))
+            dispatch(at, link)
             continue
-        events.append((at, k, level, way, s, j))
+        steps.append((at, 0, what))
         if (s + 1, j) in ring.slots[way]:
-            push(at, (False, k, level, way, s + 1, j))
+            push(at, "ready", (k, level, way, s + 1, j))
         if level == 0:
             seen.setdefault(k, set()).add((way, s, j))
             index = ring.completes(way, s, seen[k])
             for w in (0, 1):
                 if index is not None and (1, index) in outer[k].slots[w]:
-                    push(at, (False, k, 1, w, 1, index))
-    return events
+                    push(at, "ready", (k, 1, w, 1, index))
+    return sorted(steps)
 
 
 def halo_count():
@@ -300,9 +319,6 @@
     settle(fb, ls.at[0])
     settle(cb_, ls.at[1])
     each(8, lambda cb: halo1.cut(cb, fb[cb].astype(F32), stage))
-    halo1.start()
-    for peer in dps:
-        remote(par, pars.at[dp], ps.at[0], ps.at[1], peer).start()
     rz[z] = rawz[...]
     ry[y] = rawy[...]
     zbias[z] = bia[...]
@@ -338,19 +354,13 @@
     def go(copy):
         copy.start()
 
-    seen = [set(), set(), set()]
-
-    def arrive(k, level, way, s, j):
+    def perform(kind, what):
+        k, level, way, s, j = what
         ring = (inner, outer)[level][k]
-        ring.landed(way, s, j).wait()
-        if (s + 1, j) in ring.slots[way]:
-            go(ring.copy(way, s + 1, j))
-        if level == 0:
-            seen[k].add((way, s, j))
-            index = ring.completes(way, s, seen[k])
-            for w in (0, 1):
-                if index is not None and (1, index) in outer[k].slots[w]:
-                    go(outer[k].copy(w, 1, index))
+        if kind == 0:
+            ring.landed(way, s, j).wait()
+        else:
+            go(ring.copy(way, s, j))
 
     ship = [remote(act.at[a, core], act.at[a, core], as_.at[a], ar.at[a], sibling) for a in range(2)]
 
@@ -482,7 +492,7 @@
                 piece = value[:, :, 128 * cb : 128 * cb + 128]
                 acc[m, :, cb] = piece if n == 0 else acc[m, :, cb] + piece
 
-    tasks = [(0.3, 0.5, None, bias_push), (0.6, 1.5, None, params), (1.2, 2.5, None, borders)]
+    tasks = [(0.3, 0.5, None, bias_push), (0.6, 5.0, None, params), (1.2, 9.0, None, borders)]
     tasks += [(0.6, 0.0, None, functools.partial(conv_piece, i)) for i in range(4)]
     tasks += [(0.8, 0.0, None, norm), (0.6, 0.0, None, biases)]
     for n in range(LAST):
@@ -499,11 +509,14 @@
                 go(inner[k].copy(way, 1, j))
         for way in (0, 1):
             go(outer[k].copy(way, 1, 0))
+    halo1.start()
+    for peer in dps:
+        remote(par, pars.at[dp], ps.at[0], ps.at[1], peer).start()
     events = plan(outer, inner, (0.0, 0.3, 0.6))
 
     def needs(event, blocks):
-        _, k, level, way, s, j = event
-        if blocks is None:
+        _, kind, (k, level, way, s, j) = event
+        if blocks is None or kind:
             return False
         for kk, off in blocks:
             if kk != k:
@@ -520,7 +533,7 @@
         if events and (events[0][0] <= clock or not ready or clock < tasks[0][1]):
             event = events.pop(0)
             clock = max(clock, event[0])
-            arrive(*event[1:])
+            perform(*event[1:])
         else:
             length, _, _, piece = tasks.pop(0)
             piece()
@@ -601,10 +614,6 @@
     block_grad(mine)
     r1[mine] = sums[mine]
     each(8, lambda cb: halo2.cut(cb, bc[cb].reshape(8, 16, 128), stage))
-    halo2.start()
-    for cb in range(8):
-        pltpu.make_async_copy(ob.at[0, cb], block_out.at[:, pl.ds(128 * cb, 128)], os_.at[0]).start()
-
     def conv_back(low_, count):
         def one(i):
             cb = i + low_
@@ -621,20 +630,21 @@
     for k in range(7):
         remote(mid.at[turned(z, k + 1, 8)], r2.at[z], ts.at[2], ts.at[3], zps[k]).start()
     r2[z] = mid[z]
-    halo2.finish()
-    conv_back(0, 3)
+    halo2.start()
+    for cb in range(8):
+        pltpu.make_async_copy(ob.at[0, cb], block_out.at[:, pl.ds(128 * cb, 128)], os_.at[0]).start()
     settle(r2.at[0:7], ts.at[3])
     low[...] = jnp.sum(r2[...], axis=0)
     for k in range(7):
         remote(low, r3.at[member], ts.at[4], ts.at[5], thirds[k]).start()
     r3[member] = low[...]
-    conv_back(3, 3)
     settle(r3.at[0:7], ts.at[5])
     fin[...] = jnp.sum(r3[...], axis=0)
     for k in range(7):
         remote(fin, tot.at[z], ts.at[6], ts.at[7], zps[k]).start()
     tot[z] = fin[...]
-    conv_back(6, 2)
+    halo2.finish()
+    conv_back(0, 8)
     settle(r1.at[0:7], ts.at[0])
     for k, ref in enumerate((g0.at[0, 0:3], g1.at[0, 0:7], g2.at[0, 0:3], g0.at[0:7], g1.at[0:3], g2.at[0:7])):
         settle(ref, rs.at[k])

time: 101 us -> 96.8 us (0.958)
  the two profiles are of different devices: /device:TPU:8 before, /device:TPU:2 now
where the time goes in v5:
time: 96.8 us; the launch traced here: 96.6 us
  Pallas kernels  96 us (99%)
    pallas_call x1, Pallas kernels, whole(): pl.pallas_call(whole_body, out_shape=(jax.ShapeDtypeStruct((128, 1024), B...  94.1 us

profile of v5, /device:TPU:2, one launch (start us, length us, event | category | flops | bytes accessed | tf_op | source)
XLA Modules:
  0.0 96.6 jit_solution(4244620984003360180)
XLA Ops:
  0.6 94.1 %whole.1 = (bf16[128,1024]{1,0:T(8,128)(2,1)}, bf16[128,1024]{1,0:T(8,128)(2,1)}, f32[56,64]{1,0:T(8,128)}) custom-call(bf16[8,16,1024]{2,1,0:T(8,128)(2,1)} %bitcast.14, bf16[128,1024]{1,0:T(8,128)(2,1)} %bitcast.15, bf16[6,1024]{1,0:T(8,128)(2,1)} %w_in.1, bf16[6,1024]{1,0:T(8,128)(2,1)} %w_out.1, bf16[1,6]{1,0:T(2,128)(2,1)} %bitcast.16, ...), custom_call_target="tpu_custom_call" | custom-call | tf_op jit(solution)/shard_map/whole/pallas_call | solution.py:684
  94.8 1.9 %hand_out.1 = (bf16[128,1024]{1,0:T(8,128)(2,1)}, bf16[128,1024]{1,0:T(8,128)(2,1)}, f32[49,64]{1,0:T(8,128)}, f32[1,64]{1,0:T(1,128)}, f32[1,64]{1,0:T(1,128)}, /*index=5*/f32[1,64]{1,0:T(1,128)}, f32[1,64]{1,0:T(1,128)}) custom-call(bf16[128,1024]{1,0:T(8,128)(2,1)} %get-tuple-element.17.block_in, bf16[128,1024]{1,0:T(8,128)(2,1)} %get-tuple-element.18.grad_in, ...), custom_call_target="tpu_custom_call" | custom-call | tf_op jit(solution)/shard_map/hand_out/pallas_call | solution.py:728

commit v6 on v5

--- a/solution.py
+++ b/solution.py
@@ -294,9 +294,9 @@
         pltpu.make_async_copy(ref, ref, sem).wait()
 
     rows_in, rows_out = w_in[...].astype(F32), w_out[...].astype(F32)
-    raw[0, 0:4, :], raw[0, 4:8, :] = rows_in[0:4], rows_out[0:4]
-    raw[1, 0:2, :], raw[1, 2:4, :] = rows_in[4:6], rows_out[4:6]
-    raw[1, 4:8, :] = jnp.zeros((4, 1024), F32)
+    raw[0, 0:2, :], raw[0, 2:4, :] = rows_in[0:2], rows_out[0:2]
+    raw[0, 4:8, :] = jnp.zeros((4, 1024), F32)
+    raw[1, 0:4, :], raw[1, 4:8, :] = rows_in[2:6], rows_out[2:6]
     rawz[...] = raw[0].astype(BF16)
     rawy[...] = raw[1].astype(BF16)
     bia[...] = jnp.zeros((1, 128), F32)
@@ -343,12 +343,12 @@
     zr_, zb = zps[0], zps[-1]
     inner = [
         Ring("x", 4, 2, OFF4, lambda b, j: g0.at[y, turned(x, b, 4), pl.ds(4 * j, 4)], (xr, xb), rs.at[0], q0r, 0.7),
-        Ring("y", 8, 2, OFF8, lambda b, j: g1.at[x, turned(y, b, 8), pl.ds(4 * j, 4)], (yr, yb), rs.at[1], q1r, 0.7),
+        Ring("z", 8, 2, OFF8, lambda b, j: g1.at[x, turned(z, b, 8), pl.ds(4 * j, 4)], (zr_, zb), rs.at[1], q1r, 0.7),
         Ring("x", 4, 2, OFF4, lambda b, j: g2.at[z, turned(x, b, 4), pl.ds(4 * j, 4)], (xr, xb), rs.at[2], q2r, 0.7),
     ]
     outer = [
         Ring("y", 8, 4, OFF4, lambda b, j: g0.at[turned(y, b, 8), turned(x, OFF4[j], 4)], (yr, yb), rs.at[3], r0r, 1.4),
-        Ring("x", 4, 8, OFF8, lambda b, j: g1.at[turned(x, b, 4), turned(y, OFF8[j], 8)], (xr, xb), rs.at[4], r1r, 1.4),
+        Ring("x", 4, 8, OFF8, lambda b, j: g1.at[turned(x, b, 4), turned(z, OFF8[j], 8)], (xr, xb), rs.at[4], r1r, 1.4),
         Ring("z", 8, 4, OFF4, lambda b, j: g2.at[turned(z, b, 8), turned(x, OFF4[j], 4)], (zr_, zb), rs.at[5], r2r, 1.4),
     ]
     def go(copy):
@@ -435,8 +435,8 @@
 
         t0 = pick(j == 6 * ((l >> 1) & 7) + (l & 1))
         table[0] = jnp.sum(jnp.where(bx == (l64 >> 4), t0, 0.0), axis=0)
-        t1_ = pick(j == 6 * ((l >> 1) & 7) + 2 + (l & 1))
-        table[1, 0:4, :] = jnp.sum(jnp.where(by == (bl >> 4), t1_, 0.0), axis=1)
+        t1_ = pick(j == 6 * (l >> 4) + 2 + (l & 1))
+        table[1, 0:4, :] = jnp.sum(jnp.where(by == ((bl >> 1) & 7), t1_, 0.0), axis=1)
         for zz in range(8):
             t2_ = pick(j == 6 * zz + 4 + (l & 1))
             kept = jnp.where((bx == (l64 >> 4)) & (by == ((bl >> 1) & 7)), t2_, 0.0)
@@ -498,11 +498,11 @@
     for n in range(LAST):
         tasks.append((1.0, 0.0, CHUNKS[n], functools.partial(chunk_front, n)))
         tasks.append((0.8, 0.0, CHUNKS[n], functools.partial(chunk_back, n)))
-    home = (g0.at[y, x], g1.at[x, y], g2.at[z, x])
-    for k, (got, first_row, step) in enumerate(((rz, 0, 4), (rz, 2, 4), (ry, 0, 2))):
-        if k != 1:
-            settle((rz, ry)[k // 2].at[0:7], fs.at[k])
-            settle((rz, ry)[k // 2].at[0:7], fs.at[k + 1])
+    home = (g0.at[y, x], g1.at[x, z], g2.at[z, x])
+    for k, (got, first_row, step) in enumerate(((rz, 0, 2), (ry, 0, 4), (ry, 2, 4))):
+        if k != 2:
+            settle(got.at[0:7], fs.at[2 * k])
+            settle(got.at[0:7], fs.at[2 * k + 1])
         put(home[k], tiles(got, first_row, step))
         for way in (0, 1):
             for j in range(2):
@@ -512,7 +512,7 @@
     halo1.start()
     for peer in dps:
         remote(par, pars.at[dp], ps.at[0], ps.at[1], peer).start()
-    events = plan(outer, inner, (0.0, 0.3, 0.6))
+    events = plan(outer, inner, (0.0, 0.3, 0.3))
 
     def needs(event, blocks):
         _, kind, (k, level, way, s, j) = event

time: 96.8 us -> 96.4 us (level)
  the two profiles are of different devices: /device:TPU:2 before, /device:TPU:1 now
where the time goes in v6:
time: 96.4 us; the launch traced here: 96.2 us
  Pallas kernels  95.6 us (99%)
    pallas_call x1, Pallas kernels, whole(): pl.pallas_call(whole_body, out_shape=(jax.ShapeDtypeStruct((128, 1024), B...  93.7 us

profile of v6, /device:TPU:1, one launch (start us, length us, event | category | flops | bytes accessed | tf_op | source)
XLA Modules:
  0.0 96.2 jit_solution(14761403590393723896)
XLA Ops:
  0.6 93.7 %whole.1 = (bf16[128,1024]{1,0:T(8,128)(2,1)}, bf16[128,1024]{1,0:T(8,128)(2,1)}, f32[56,64]{1,0:T(8,128)}) custom-call(bf16[8,16,1024]{2,1,0:T(8,128)(2,1)} %bitcast.14, bf16[128,1024]{1,0:T(8,128)(2,1)} %bitcast.15, bf16[6,1024]{1,0:T(8,128)(2,1)} %w_in.1, bf16[6,1024]{1,0:T(8,128)(2,1)} %w_out.1, bf16[1,6]{1,0:T(2,128)(2,1)} %bitcast.16, ...), custom_call_target="tpu_custom_call" | custom-call | tf_op jit(solution)/shard_map/whole/pallas_call | solution.py:684
  94.4 1.9 %hand_out.1 = (bf16[128,1024]{1,0:T(8,128)(2,1)}, bf16[128,1024]{1,0:T(8,128)(2,1)}, f32[49,64]{1,0:T(8,128)}, f32[1,64]{1,0:T(1,128)}, f32[1,64]{1,0:T(1,128)}, /*index=5*/f32[1,64]{1,0:T(1,128)}, f32[1,64]{1,0:T(1,128)}) custom-call(bf16[128,1024]{1,0:T(8,128)(2,1)} %get-tuple-element.17.block_in, bf16[128,1024]{1,0:T(8,128)(2,1)} %get-tuple-element.18.grad_in, ...), custom_call_target="tpu_custom_call" | custom-call | tf_op jit(solution)/shard_map/hand_out/pallas_call | solution.py:728

commit v7 on v6

--- a/solution.py
+++ b/solution.py
@@ -256,7 +256,7 @@
     block_out, grad_in, out_sums,
     fb, cb_, raw, rawz, rawy, slab, par, bia, ecol, ecor, stage, hrows, hcols, hcors, wrows, wcols, wcors, pad, bpad, pars, taps, row, zbias, bias, table,
     rz, ry, g0, g1, g2, act, hid, acc, part, mypart, conv, inv, bc, wire, ob, sums,
-    r1, r2, r3, mid, low, fin, tot,
+    sent, r1, r2, r3, mid, low, fin, tot,
     ls, hs, hr, h2r, ps, zs, bs, as_, ar, fs, q0r, q1r, q2r, r0r, r1r, r2r, rs, es, er, ts, os_,
 ):
     x, y, z, core = place()
@@ -601,18 +601,19 @@
     def firsts(k):
         other = lax.rem(mine + k, 8)
         peer = device(lax.rem(other, 2) * 2 + xl, yh * 4 + lax.div(other, 2), z, core)
-        return other, remote(sums.at[other], r1.at[mine], ts.at[0], ts.at[1], peer)
+        return other, remote(sent.at[other], r1.at[mine], ts.at[0], ts.at[1], peer)
 
     def grad_step(i):
         other, copy = firsts(i + 1)
         rear(other)
         block_grad(other)
+        sent[other] = sums[other].astype(BF16)
         copy.start()
 
     each(7, grad_step)
     rear(mine)
     block_grad(mine)
-    r1[mine] = sums[mine]
+    r1[mine] = sums[mine].astype(BF16)
     each(8, lambda cb: halo2.cut(cb, bc[cb].reshape(8, 16, 128), stage))
     def conv_back(low_, count):
         def one(i):
@@ -626,7 +627,7 @@
             pltpu.make_async_copy(ob.at[1, cb], grad_in.at[:, pl.ds(128 * cb, 128)], os_.at[1]).start()
 
     settle(r1.at[0:7], ts.at[1])
-    mid[...] = jnp.sum(r1[...], axis=0).reshape(8, 8, 128)
+    mid[...] = jnp.sum(r1[...].astype(F32), axis=0).reshape(8, 8, 128)
     for k in range(7):
         remote(mid.at[turned(z, k + 1, 8)], r2.at[z], ts.at[2], ts.at[3], zps[k]).start()
     r2[z] = mid[z]
@@ -676,7 +677,7 @@
         ((2, 2, 128, 1024), BF16), ((2, 256, 256), BF16), ((2, 2, 8, 128, 128), F32),
         ((2, 8, 128, 128), BF16), ((2, 8, 128, 128), BF16), ((8, 128, 128), F32), ((128, 128), F32),
         ((8, 128, 128), F32), ((8, 8, 16, 128), BF16), ((2, 8, 128, 128), BF16), ((8, 64, 128), F32),
-        ((8, 64, 128), F32), ((8, 8, 128), F32), ((8, 8, 128), F32), ((8, 8, 128), F32), ((8, 128), F32), ((8, 128), F32),
+        ((8, 64, 128), BF16), ((8, 64, 128), BF16), ((8, 8, 128), F32), ((8, 8, 128), F32), ((8, 8, 128), F32), ((8, 128), F32), ((8, 128), F32),
         ((8, 8, 128), F32),
     ]
     sems = [(2,), (8,), (8,), (8,), (2,), (2,), (2,), (2,), (2,), (4,), (2, 3), (2, 7), (2, 3), (2, 14), (2, 12), (2, 14)]

time: 96.4 us -> 90.1 us (0.935)
  the two profiles are of different devices: /device:TPU:1 before, /device:TPU:8 now
where the time goes in v7:
time: 90.1 us; the launch traced here: 89.8 us
  Pallas kernels  89.2 us (99%)
    pallas_call x1, Pallas kernels, whole(): pl.pallas_call(whole_body, out_shape=(jax.ShapeDtypeStruct((128, 1024), B...  87.3 us
    pallas_call x1, Pallas kernels, per_device(): pl.pallas_call(hand_out, out_shape=[jax.ShapeDtypeStruct((pixels, width),...  1.85 us

profile of v7, /device:TPU:8, one launch (start us, length us, event | category | flops | bytes accessed | tf_op | source)
XLA Modules:
  0.0 89.8 jit_solution(17989532110263485263)
XLA Ops:
  0.6 87.3 %whole.1 = (bf16[128,1024]{1,0:T(8,128)(2,1)}, bf16[128,1024]{1,0:T(8,128)(2,1)}, f32[56,64]{1,0:T(8,128)}) custom-call(bf16[8,16,1024]{2,1,0:T(8,128)(2,1)} %bitcast.14, bf16[128,1024]{1,0:T(8,128)(2,1)} %bitcast.15, bf16[6,1024]{1,0:T(8,128)(2,1)} %w_in.1, bf16[6,1024]{1,0:T(8,128)(2,1)} %w_out.1, bf16[1,6]{1,0:T(2,128)(2,1)} %bitcast.16, ...), custom_call_target="tpu_custom_call" | custom-call | tf_op jit(solution)/shard_map/whole/pallas_call | solution.py:685
  88.0 1.9 %hand_out.1 = (bf16[128,1024]{1,0:T(8,128)(2,1)}, bf16[128,1024]{1,0:T(8,128)(2,1)}, f32[49,64]{1,0:T(8,128)}, f32[1,64]{1,0:T(1,128)}, f32[1,64]{1,0:T(1,128)}, /*index=5*/f32[1,64]{1,0:T(1,128)}, f32[1,64]{1,0:T(1,128)}) custom-call(bf16[128,1024]{1,0:T(8,128)(2,1)} %get-tuple-element.17.block_in, bf16[128,1024]{1,0:T(8,128)(2,1)} %get-tuple-element.18.grad_in, ...), custom_call_target="tpu_custom_call" | custom-call | tf_op jit(solution)/shard_map/hand_out/pallas_call | solution.py:729
